TPU v7x, 32 devices: a whole 2x2x4 slice. The times are simulated.
32 devices in a mesh: group: 2 (over x), shard: 16 (over z, y, core).
Axes of the slice: x: 2, y: 2, z: 4, core: 2. Of those that a mesh axis runs over, the one named last changes fastest.
Arguments:
- rollout_rows: bfloat16 [512, 8192], P('group', 'shard'), may hold values from -6 to 6
- assign: int32 [512], replicated, may hold values from 0 to 511, each once
- cotangent: bfloat16 [512, 8192], P('group', 'shard'), may hold values from -3 to 3
- w_master: float32 [8192, 8192], P('group', 'shard'), may hold values from -0.0625 to 0.0625
- adam_m: float32 [8192, 8192], P('group', 'shard'), may hold values from -6 to 6
- adam_v: float32 [8192, 8192], P('group', 'shard'), may hold values from 0.05 to 1
- tile_mask: int32 [64, 64], replicated, may hold values from 0 to 1, as said below
Outputs:
- projected: bfloat16 [512, 8192], P('group', 'shard')
- input_grad: bfloat16 [512, 8192], P('group', 'shard')
- w_updated: float32 [8192, 8192], P('group', 'shard')
- m_updated: float32 [8192, 8192], P('group', 'shard')
- v_updated: float32 [8192, 8192], P('group', 'shard')
- rollout_tiles: bfloat16 [64, 6, 128, 128], P('shard')
Inputs may be any that keep to these rules, and one draw needn't show every extreme that they name: `tile_mask`: each tile column has 1 to 6 trainable tiles, and some column has exactly 6. `assign`: a permutation of the 512 rollout rows.
All inputs are finite; a program needn't handle non-finite values.
Results may differ from a plain program's by a relative error of at most 0.0051.
Values may be sent and summed in bfloat16 or wider, within the bound.
No kernel may reach another device: no remote copies, remote signals or barrier semaphores. Data moves between devices by JAX's collectives and lax.ppermute only.
A program may use at most 192 MiB of HBM per device.

v0:
```python
import functools

import jax
import jax.numpy as jnp
from jax import lax
from jax.experimental import pallas as pl
from jax.experimental.pallas import tpu as pltpu
from jax.sharding import PartitionSpec as P


TILE = 128
CAP = 6


beta_one = 0.9
beta_two = 0.999
learn_rate = 0.02
eps_adam = 1e-08
bias_one = 1.0 - 0.9**10
bias_two = 1.0 - 0.999**10


def cast_kernel(order, w_ref, *refs):
    copy_ref, half_ref = refs[-2:]
    w = w_ref[...]
    copy_ref[...] = w
    half_ref[...] = w.astype(jnp.bfloat16)


def cast_pass(blocks, order, first=0, after=()):
    count = order.shape[0] - first
    _, depth, width = blocks.shape
    take = pl.BlockSpec((1, depth, width), lambda i, order: (order[i + first], 0, 0))
    put = pl.BlockSpec((1, depth, width), lambda i, order: (i, 0, 0))
    return pl.pallas_call(
        cast_kernel,
        out_shape=(
            jax.ShapeDtypeStruct(blocks.shape, jnp.float32),
            jax.ShapeDtypeStruct((count, depth, width), jnp.bfloat16),
        ),
        grid_spec=pltpu.PrefetchScalarGridSpec(
            num_scalar_prefetch=1,
            grid=(count,),
            in_specs=[take] + [pl.BlockSpec(memory_space=pl.ANY)] * len(after),
            out_specs=(take, put),
        ),
        cost_estimate=pl.CostEstimate(
            flops=0, bytes_accessed=10 * count * depth * width, transcendentals=0
        ),
        name="cast_pass",
    )(order, blocks, *after)


def back_kernel(near_ref, other_ref, half_ref, out_ref, cot_ref):
    rows = near_ref.shape[0]

    @pl.when(pl.program_id(0) == 0)
    def _():
        cot_ref[:rows, :] = near_ref[...]
        cot_ref[rows:, :] = other_ref[...]

    out_ref[0] = lax.dot_general(
        cot_ref[...], half_ref[0], (((1,), (1,)), ((), ())), preferred_element_type=jnp.float32
    ).astype(out_ref.dtype)


def back_product(near, other, half):
    count, depth, width = half.shape
    rows = near.shape[0] + other.shape[0]
    vmem = pl.BlockSpec(memory_space=pltpu.VMEM)
    return pl.pallas_call(
        back_kernel,
        out_shape=jax.ShapeDtypeStruct((count, rows, depth), jnp.bfloat16),
        grid=(count,),
        in_specs=[vmem, vmem, pl.BlockSpec((1, depth, width), lambda i: (i, 0, 0))],
        out_specs=pl.BlockSpec((1, rows, depth), lambda i: (i, 0, 0)),
        scratch_shapes=[pltpu.VMEM((rows, width), jnp.bfloat16)],
        cost_estimate=pl.CostEstimate(
            flops=2 * count * rows * width * depth,
            bytes_accessed=2 * count * depth * (width + rows),
            transcendentals=0,
        ),
        name="back_product",
    )(near, other, half)


def weight_kernel(
    order, near_ref, other_ref, w_ref, _, copy_ref, half_ref, out_ref, cot_ref
):
    rows = near_ref.shape[0]

    @pl.when(pl.program_id(0) == 0)
    def _():
        cot_ref[:rows, :] = near_ref[...]
        cot_ref[rows:, :] = other_ref[...]

    w = w_ref[0]
    copy_ref[0] = w
    half = w.astype(jnp.bfloat16)
    half_ref[0] = half
    out_ref[0] = lax.dot_general(
        cot_ref[...], half, (((1,), (1,)), ((), ())), preferred_element_type=jnp.float32
    ).astype(out_ref.dtype)


def turn_kernel(near_ref, other_ref, turn_ref, out_ref):
    rows = near_ref.shape[0]
    place = lax.broadcasted_iota(jnp.int32, (2 * rows, 2 * rows), 0)
    chosen = (place == turn_ref[...]).astype(jnp.bfloat16)
    cot = jnp.concatenate([near_ref[...], other_ref[...]], axis=0)
    out_ref[...] = jnp.dot(chosen, cot, preferred_element_type=jnp.float32).astype(jnp.bfloat16)


def turn_rows(near, other, turn):
    rows, width = near.shape
    vmem = pl.BlockSpec(memory_space=pltpu.VMEM)
    return pl.pallas_call(
        turn_kernel,
        out_shape=jax.ShapeDtypeStruct((2 * rows, width), jnp.bfloat16),
        in_specs=[vmem] * 3,
        out_specs=vmem,
        cost_estimate=pl.CostEstimate(
            flops=8 * rows * rows * width, bytes_accessed=8 * rows * width, transcendentals=0
        ),
        name="turn_rows",
    )(near, other, turn)


def weight_pass(near, other, blocks, order, count, copied):
    width = near.shape[1]
    rows = near.shape[0] + other.shape[0]
    depth = blocks.shape[1]
    vmem = pl.BlockSpec(memory_space=pltpu.VMEM)
    take = pl.BlockSpec((1, depth, width), lambda i, order: (order[i], 0, 0))
    put = pl.BlockSpec((1, depth, width), lambda i, order: (i, 0, 0))
    out = pl.BlockSpec((1, rows, depth), lambda i, order: (i, 0, 0))
    return pl.pallas_call(
        weight_kernel,
        out_shape=(
            jax.ShapeDtypeStruct(blocks.shape, jnp.float32),
            jax.ShapeDtypeStruct((count, depth, width), jnp.bfloat16),
            jax.ShapeDtypeStruct((count, rows, depth), jnp.bfloat16),
        ),
        grid_spec=pltpu.PrefetchScalarGridSpec(
            num_scalar_prefetch=1,
            grid=(count,),
            in_specs=[vmem, vmem, take, pl.BlockSpec(memory_space=pl.ANY)],
            out_specs=(take, put, out),
            scratch_shapes=[pltpu.VMEM((rows, width), jnp.bfloat16)],
        ),
        input_output_aliases={4: 0},
        cost_estimate=pl.CostEstimate(
            flops=2 * count * rows * width * depth,
            bytes_accessed=count * depth * (10 * width + 2 * rows),
            transcendentals=0,
        ),
        name="weight_pass",
    )(order, near, other, blocks, copied)


def forward_kernel(x_ref, w_ref, out_ref):
    product = jnp.dot(x_ref[0], w_ref[0], preferred_element_type=jnp.float32)

    @pl.when(pl.program_id(0) == 0)
    def _():
        out_ref[...] = product

    @pl.when(pl.program_id(0) > 0)
    def _():
        out_ref[...] += product


def forward_product(x, half):
    count, rows, depth = x.shape
    width = half.shape[2]
    return pl.pallas_call(
        forward_kernel,
        out_shape=jax.ShapeDtypeStruct((rows, width), jnp.float32),
        grid=(count,),
        in_specs=[
            pl.BlockSpec((1, rows, depth), lambda i: (i, 0, 0)),
            pl.BlockSpec((1, depth, width), lambda i: (i, 0, 0)),
        ],
        out_specs=pl.BlockSpec((rows, width), lambda i: (0, 0)),
        cost_estimate=pl.CostEstimate(
            flops=2 * count * rows * width * depth,
            bytes_accessed=2 * count * depth * (rows + width),
            transcendentals=0,
        ),
        name="forward_product",
    )(x, half)


def tile_kernel(slots, count, sides, owned, row, piece, lane, *refs):
    x_refs = refs[: count * sides]
    (
        cot_ref, w_in, m_in, v_in, w_out, m_out, v_out, fresh_ref,
        w_buf, m_buf, v_buf, x_buf, load_sem, x_sem, store_sem,
    ) = refs[count * sides :]
    parts = ((w_in, w_buf), (m_in, m_buf), (v_in, v_buf))
    rows = x_refs[0].shape[0]

    def window(ref, i):
        return ref.at[
            pl.ds(pl.multiple_of(row[i] * TILE, TILE), TILE),
            pl.ds(pl.multiple_of(i // CAP * TILE, TILE), TILE),
        ]

    def load(i, k):
        source, buf = parts[k]
        return pltpu.make_async_copy(window(source, i), buf.at[i], load_sem.at[k, i])

    def store(i, k):
        target = (window(w_out, i), m_out.at[i], v_out.at[i])[k]
        return pltpu.make_async_copy(parts[k][1].at[i], target, store_sem.at[k, i])

    def fetch(i, n, side):
        return pltpu.make_async_copy(
            x_refs[n * sides + side].at[:, pl.ds(pl.multiple_of(lane[i] * TILE, TILE), TILE)],
            x_buf.at[i, pl.ds(side * rows, rows), :],
            x_sem.at[side, i],
        )

    @pl.loop(0, slots)
    def _(i):
        @pl.when(owned[i] > 0)
        def _():
            for n in range(count):

                @pl.when(piece[i] == n)
                def _():
                    for side in range(sides):
                        fetch(i, n, side).start()

            for k in range(3):
                load(i, k).start()

    @pl.loop(0, slots)
    def _(i):
        @pl.when(owned[i] > 0)
        def _():
            for side in range(sides):
                fetch(i, 0, side).wait()
            cot = cot_ref[:, pl.ds(pl.multiple_of(i // CAP * TILE, TILE), TILE)]
            gradient = lax.dot_general(
                x_buf[i], cot, (((0,), (0,)), ((), ())), preferred_element_type=jnp.float32
            )
            for k in range(3):
                load(i, k).wait()
            m = beta_one * m_buf[i] + (1.0 - beta_one) * gradient
            v = beta_two * v_buf[i] + (1.0 - beta_two) * gradient * gradient
            step = m / bias_one / (jnp.sqrt(v / bias_two) + eps_adam)
            w = w_buf[i] - learn_rate * step
            w_buf[i], m_buf[i], v_buf[i] = w, m, v
            fresh_ref[i] = w.astype(jnp.bfloat16)
            for k in range(3):
                store(i, k).start()

        @pl.when(owned[i] == 0)
        def _():
            fresh_ref[i] = jnp.zeros((TILE, TILE), jnp.bfloat16)

    @pl.loop(0, slots)
    def _(i):
        @pl.when(owned[i] > 0)
        def _():
            for k in range(3):
                store(i, k).wait()


def update_tiles(owned, row, piece, lane, x_parts, count, cot, w, m, v):
    slots = owned.shape[0]
    sides = len(x_parts) // count
    smem = pl.BlockSpec(memory_space=pltpu.SMEM)
    vmem = pl.BlockSpec(memory_space=pltpu.VMEM)
    hbm = pl.BlockSpec(memory_space=pl.ANY)
    state = jax.ShapeDtypeStruct((slots, TILE, TILE), jnp.float32)
    buf = pltpu.VMEM((slots, TILE, TILE), jnp.float32)
    sems = pltpu.SemaphoreType.DMA((3, slots))
    return pl.pallas_call(
        functools.partial(tile_kernel, slots, count, sides),
        out_shape=(
            jax.ShapeDtypeStruct(w.shape, w.dtype),
            state,
            state,
            jax.ShapeDtypeStruct(state.shape, jnp.bfloat16),
        ),
        in_specs=[smem] * 4 + [vmem] * (len(x_parts) + 1) + [hbm] * 3,
        out_specs=(hbm, hbm, hbm, vmem),
        scratch_shapes=[buf, buf, buf, pltpu.VMEM((slots, cot.shape[0], TILE), jnp.bfloat16)]
        + [sems, pltpu.SemaphoreType.DMA((sides, slots)), sems],
        input_output_aliases={5 + len(x_parts): 0},
        cost_estimate=pl.CostEstimate(
            flops=2 * slots * TILE * TILE * cot.shape[0],
            bytes_accessed=26 * slots * TILE * TILE,
            transcendentals=slots * TILE * TILE,
        ),
        name="update_tiles",
    )(owned, row, piece, lane, *x_parts, cot, w, m, v)


CHUNKS = 8
DEPTH = 8


def finish_steps(slots, owned, row, a_ref, new_ref, out_ref, ring, tiles, sems, work):
    in_sem, out_sem, tile_sem = sems
    height = ring.shape[1]

    def load(c):
        source = a_ref.at[pl.ds(c * height, height), :]
        return pltpu.make_async_copy(source, ring.at[c % DEPTH], in_sem.at[c % DEPTH])

    def store(c):
        target = out_ref.at[pl.ds(c * height, height), :]
        return pltpu.make_async_copy(ring.at[c % DEPTH], target, out_sem.at[c % DEPTH])

    def fetch(i):
        return pltpu.make_async_copy(new_ref.at[i], tiles.at[i], tile_sem.at[i])

    def put(i):
        target = out_ref.at[
            pl.ds(pl.multiple_of(row[i] * TILE, TILE), TILE),
            pl.ds(pl.multiple_of(i // CAP * TILE, TILE), TILE),
        ]
        return pltpu.make_async_copy(tiles.at[i], target, tile_sem.at[i])

    def each(do):
        @pl.loop(0, slots)
        def _(i):
            @pl.when(owned[i] > 0)
            def _():
                do(i)

    for c in range(min(DEPTH, CHUNKS)):
        load(c).start()
    each(lambda i: fetch(i).start())
    waited = 0
    for c in range(CHUNKS):
        if c >= 2 and c - 2 + DEPTH < CHUNKS:
            store(c - 2).wait()
            waited = c - 1
            load(c - 2 + DEPTH).start()
        load(c).wait()
        store(c).start()
        if c < len(work):
            work[c]()
    each(lambda i: fetch(i).wait())
    for c in range(waited, CHUNKS):
        store(c).wait()
    each(lambda i: put(i).start())
    for step in work[CHUNKS:]:
        step()
    each(lambda i: put(i).wait())


def product_steps(count, x_refs, w_ref, base_ref, sum_ref):
    rows = x_refs[0].shape[0]

    def step(k):
        n, side = divmod(k, 2)
        into = pl.ds(side * rows, rows)
        product = jnp.dot(x_refs[k][...], w_ref[n], preferred_element_type=jnp.float32)
        if n > 0:
            sum_ref[into, :] += product
        elif base_ref is not None:
            sum_ref[into, :] = base_ref[into, :] + product
        else:
            sum_ref[into, :] = product

    return [functools.partial(step, k) for k in range(2 * count)]


def low_kernel(slots, count, owned, row, *refs):
    w_ref, a_ref, new_ref, sum_ref, out_ref, ring, tiles, *sems = refs[2 * count :]
    work = product_steps(count, refs[: 2 * count], w_ref, None, sum_ref)
    finish_steps(slots, owned, row, a_ref, new_ref, out_ref, ring, tiles, sems, work)


def turned_kernel(count, *refs):
    w_ref, base_ref, turn_ref, mine_ref, give_ref, sum_ref = refs[2 * count :]
    for step in product_steps(count, refs[: 2 * count], w_ref, base_ref, sum_ref):
        step()
    total, rows = sum_ref.shape[0], mine_ref.shape[0]
    place = lax.broadcasted_iota(jnp.int32, (total, rows), 0)

    def rows_of(side, values):
        chosen = place == turn_ref[:, side * rows : (side + 1) * rows]
        return lax.dot_general(
            chosen.astype(jnp.bfloat16), values, (((0,), (0,)), ((), ())),
            preferred_element_type=jnp.float32,
        )

    value = sum_ref[...]
    head = value.astype(jnp.bfloat16)
    rest = (value - head.astype(jnp.float32)).astype(jnp.bfloat16)
    give_ref[...] = rows_of(1, head).astype(jnp.bfloat16)
    mine_ref[...] = rows_of(0, head) + rows_of(0, rest)


def turned_product(parts, half, base, turn):
    count = half.shape[0]
    rows, depth = parts[0].shape
    width = half.shape[2]
    vmem = pl.BlockSpec(memory_space=pltpu.VMEM)
    return pl.pallas_call(
        functools.partial(turned_kernel, count),
        out_shape=(
            jax.ShapeDtypeStruct((rows, width), jnp.float32),
            jax.ShapeDtypeStruct((rows, width), jnp.bfloat16),
        ),
        in_specs=[vmem] * (2 * count + 3),
        out_specs=(vmem, vmem),
        scratch_shapes=[pltpu.VMEM((2 * rows, width), jnp.float32)],
        cost_estimate=pl.CostEstimate(
            flops=4 * count * rows * width * depth,
            bytes_accessed=2 * count * depth * (2 * rows + width),
            transcendentals=0,
        ),
        name="turned_product",
    )(*parts, half, base, turn)


def plain_kernel(slots, owned, row, a_ref, new_ref, out_ref, ring, tiles, *sems):
    finish_steps(slots, owned, row, a_ref, new_ref, out_ref, ring, tiles, sems, [])


def finish_state(owned, row, a, new, parts=(), half=None):
    slots = owned.shape[0]
    count = len(parts) // 2
    smem = pl.BlockSpec(memory_space=pltpu.SMEM)
    vmem = pl.BlockSpec(memory_space=pltpu.VMEM)
    hbm = pl.BlockSpec(memory_space=pl.ANY)
    outs, operands, scratch = [], list(parts), []
    kernel = functools.partial(plain_kernel, slots)
    if parts:
        operands.append(half)
        kernel = functools.partial(low_kernel, slots, count)
        outs = [jax.ShapeDtypeStruct((2 * parts[0].shape[0], half.shape[2]), jnp.float32)]
    scratch += [
        pltpu.VMEM((DEPTH, a.shape[0] // CHUNKS, a.shape[1]), a.dtype),
        pltpu.VMEM((slots, TILE, TILE), a.dtype),
        pltpu.SemaphoreType.DMA((DEPTH,)),
        pltpu.SemaphoreType.DMA((DEPTH,)),
        pltpu.SemaphoreType.DMA((slots,)),
    ]
    flops = sum(2 * p.size * half.shape[2] for p in parts)
    return pl.pallas_call(
        kernel,
        out_shape=outs + [jax.ShapeDtypeStruct(a.shape, a.dtype)],
        in_specs=[smem, smem] + [vmem] * len(operands) + [hbm, hbm],
        out_specs=[vmem] * len(outs) + [hbm],
        scratch_shapes=scratch,
        cost_estimate=pl.CostEstimate(
            flops=flops, bytes_accessed=8 * a.size, transcendentals=0
        ),
        name="finish_state",
    )(owned, row, *operands, a, new)


def swap(a, axis, size, bit):
    return lax.ppermute(a, axis, [(i, i ^ bit) for i in range(size)])


def owned_slots(tile_mask, group_at, shard_at, row_tiles, col_tiles):
    mask_cols = lax.dynamic_slice_in_dim(tile_mask, shard_at * col_tiles, col_tiles, 1)
    count = tile_mask.shape[0]
    at = jnp.arange(count)
    before = (at[None, :] < at[:, None]).astype(jnp.float32)
    rank = jnp.dot(before, mask_cols.astype(jnp.float32)).astype(jnp.int32)
    hit = (mask_cols[:, :, None] > 0) & (rank[:, :, None] == jnp.arange(CAP)[None, None, :])
    row = jnp.sum(jnp.where(hit, at[:, None, None], 0), axis=0).reshape(-1)
    live = jnp.sum(hit.astype(jnp.int32), axis=0).reshape(-1)
    owned = jnp.where(row // row_tiles == group_at, live, 0)
    return owned, row - group_at * row_tiles


def pair_shards(groups, shard_count, rollout_rows, assign, cotangent, w_master, adam_m, adam_v, tile_mask):
    group_at = lax.axis_index("group")
    shard_at = lax.axis_index("shard")
    row_count, features = rollout_rows.shape
    width = cotangent.shape[1]
    col_tiles = width // TILE
    row_tiles = w_master.shape[0] // TILE
    half_count = shard_count // 2
    bits = [half_count >> (k + 1) for k in range(half_count.bit_length() - 1)]
    offsets = [0]
    for bit in bits:
        offsets = offsets + [o | bit for o in offsets]
    base = shard_at % half_count
    order = base ^ jnp.asarray(offsets, jnp.int32)
    in_half = shard_at // half_count == group_at

    blocks = w_master.reshape(half_count, features, width)
    low = half_count // 2

    row_total = groups * row_count
    start = group_at * row_count
    turned = jnp.where(group_at == 0, assign, jnp.concatenate([assign[row_count:], assign[:row_count]]))
    turned = jnp.where(turned >= start, turned - start, turned + row_total - start)

    owned, row = owned_slots(tile_mask, group_at, shard_at, row_tiles, col_tiles)
    per_block = features // TILE
    block = jnp.clip(row // per_block, 0, half_count - 1) ^ base
    piece = sum(jnp.where(block & bit > 0, 1 << k, 0) for k, bit in enumerate(bits))
    lane = lax.rem(row + row_tiles * groups, per_block)
    piece = piece.astype(jnp.int32)
    turn = turned.reshape(1, row_total)

    cot_other = swap(cotangent, "group", groups, 1)
    far = swap(rollout_rows, "shard", shard_count, half_count)
    w_copy, half_high = cast_pass(blocks, order, low, (owned, row, piece, lane, turn))
    sent = back_product(cotangent, cot_other, half_high)
    got = swap(sent, "shard", shard_count, bits[-1])
    keep = jnp.where(in_half, rollout_rows, far)
    give = jnp.where(in_half, far, rollout_rows)
    x_parts = [keep, swap(give, "group", groups, 1)]
    for bit in bits:
        held = list(x_parts)
        for part in held:
            x_parts.append(swap(part, "shard", shard_count, bit))

    w_copy, half_low, kept = weight_pass(cotangent, cot_other, blocks, order, low, w_copy)
    cot_turned = turn_rows(cotangent, cot_other, turn)
    terms = {
        o: kept[n].astype(jnp.float32) + got[n].astype(jnp.float32)
        for n, o in enumerate(offsets[:low])
    }
    for bit in bits[:-1]:
        for o in sorted([o for o in terms if o & bit], reverse=True):
            term = swap(terms.pop(o).astype(jnp.bfloat16), "shard", shard_count, bit)
            terms[o ^ bit] = terms[o ^ bit] + term.astype(jnp.float32)
    done = terms[0].reshape(groups, row_count, features)
    other = swap(done[1].astype(jnp.bfloat16), "group", groups, 1).astype(jnp.float32)
    near = jnp.where(in_half, done[0], other)
    away = jnp.where(in_half, other, done[0]).astype(jnp.bfloat16)
    back = swap(away, "shard", shard_count, half_count).astype(jnp.float32)
    input_grad = (near + back).astype(jnp.bfloat16)

    w_updated, m_new, v_new, fresh = update_tiles(
        owned, row, piece, lane, x_parts, half_count, cot_turned,
        w_copy.reshape(w_master.shape), adam_m, adam_v,
    )
    tiles = fresh + swap(fresh, "group", groups, 1)
    rollout_tiles = tiles.reshape(col_tiles, CAP, TILE, TILE)

    partial, m_updated = finish_state(
        owned, row, adam_m, m_new, x_parts[: 2 * low], half_low
    )
    mine, give = turned_product(x_parts[2 * low :], half_high, partial, turn)
    (v_updated,) = finish_state(owned, row, adam_v, v_new)
    taken = swap(give, "group", groups, 1).astype(jnp.float32)
    projected = (mine + taken).astype(jnp.bfloat16)
    return (projected, input_grad, w_updated, m_updated, v_updated, rollout_tiles)


def any_shards(groups, shard_count, rollout_rows, assign, cotangent, w_master, adam_m, adam_v, tile_mask):
    group_at = lax.axis_index("group")
    shard_at = lax.axis_index("shard")
    row_count, features = rollout_rows.shape
    width = cotangent.shape[1]
    col_tiles = width // TILE
    row_tiles = w_master.shape[0] // TILE
    per_group = shard_count // groups
    row_total = groups * row_count
    order = jnp.arange(per_group, dtype=jnp.int32)
    w_copy, half = cast_pass(w_master.reshape(per_group, -1, width), order)
    x_cols = lax.all_gather(rollout_rows, "group", axis=0, tiled=True)
    x_full = lax.all_gather(x_cols, "shard", axis=0)
    x_all = lax.dynamic_slice_in_dim(x_full, group_at * per_group, per_group, 0)
    cot_all = lax.all_gather(cotangent, "group", axis=0, tiled=True)
    middle = row_total // 2
    products = back_product(cot_all[:middle], cot_all[middle:], half)
    products = products.reshape(per_group, groups, row_count, features)
    products = products.transpose(1, 0, 2, 3).reshape(shard_count * row_count, features)
    summed = lax.psum_scatter(products, "shard", scatter_dimension=0, tiled=True)
    moves = [
        (g * shard_count + r * per_group + k, r * shard_count + g * per_group + k)
        for g in range(groups)
        for r in range(groups)
        for k in range(per_group)
    ]
    input_grad = lax.ppermute(summed, ("group", "shard"), moves)
    pick = (jnp.arange(row_total)[:, None] == assign[None, :]).astype(jnp.bfloat16)
    cot_turned = jnp.dot(pick, cot_all, preferred_element_type=jnp.float32).astype(jnp.bfloat16)
    partial = jnp.take(forward_product(x_all, half), assign, axis=0)
    projected = lax.psum_scatter(partial, "group", scatter_dimension=0, tiled=True)
    projected = projected.astype(jnp.bfloat16)
    owned, row = owned_slots(tile_mask, group_at, shard_at, row_tiles, col_tiles)
    per_block = features // TILE
    piece = jnp.clip(row // per_block, 0, per_group - 1)
    lane = lax.rem(row + row_tiles * groups, per_block)
    w_updated, m_new, v_new, fresh = update_tiles(
        owned, row, piece, lane, list(x_all), per_group, cot_turned,
        w_copy.reshape(w_master.shape), adam_m, adam_v,
    )
    (m_updated,) = finish_state(owned, row, adam_m, m_new)
    (v_updated,) = finish_state(owned, row, adam_v, v_new)
    rollout_tiles = lax.psum(fresh, "group").reshape(col_tiles, CAP, TILE, TILE)
    return (projected, input_grad, w_updated, m_updated, v_updated, rollout_tiles)


def solution(mesh):
    groups, shard_count = mesh.shape["group"], mesh.shape["shard"]
    paired = groups == 2 and shard_count == 16
    inner = functools.partial(pair_shards if paired else any_shards, groups, shard_count)

    placed = (
        P("group", "shard"),
        P(),
        P("group", "shard"),
        P("group", "shard"),
        P("group", "shard"),
        P("group", "shard"),
        P(),
    )
    return jax.shard_map(
        inner,
        mesh=mesh,
        in_specs=placed,
        out_specs=(
            P("group", "shard"),
            P("group", "shard"),
            P("group", "shard"),
            P("group", "shard"),
            P("group", "shard"),
            P("shard", None, None, None),
        ),
        check_vma=False,
    )
```

profile of v0, /device:TPU:0, one launch (start us, length us, event | category | flops | bytes accessed | tf_op | source)
XLA Modules:
  0.0 131.3 jit_solution(14439900637137107538)
XLA Ops:
  0.6 3.0 %collective-permute-start.16 = (bf16[256,512]{1,0:T(8,128)(2,1)}, bf16[256,512]{1,0:T(8,128)(2,1)S(1)}, u32[]{:S(2)}, u32[]{:S(2)}) collective-permute-start(bf16[256,512]{1,0:T(8,128)(2,1)} %near_ref.5), channel_id=1, source_target_pairs={{0,16},{16,0},{1,17},{17,1},{2,18},{18,2},{3,19},{19,3},{4,20},{20... | collective-permute-start | bytes 786440 | tf_op jit(solution)/shard_map/ppermute | solution.py:462
  3.8 0.1 convolution_convert_fusion
  4.0 0.8 fusion.12
  4.8 0.3 select_reduce_fusion
  5.0 0.1 copy.21
  5.2 0.1 copy.22
  5.4 1.2 broadcast_xor_fusion.order
  6.6 0.6 compare_select_fusion
  7.2 0.6 fusion.10.refs_2_.piece
  7.7 1.3 subtract_select_fusion
  9.0 6.0 %cast_pass.1 = (f32[8,512,512]{2,1,0:T(8,128)}, bf16[4,512,512]{2,1,0:T(8,128)(2,1)}) custom-call(s32[8]{0:T(128)} %broadcast_xor_fusion.order, f32[8,512,512]{2,1,0:T(8,128)} %bitcast.16, s32[24]{0:T(128)} %get-tuple-element.42.refs_0_.owned, s32[24]{0:T(128)} %copy-done.17, s32[24]{0:T(128)} %fusion.10.refs_2_.piece, s32[24]{0:T(128)} %get-tuple-element.34.refs_3_.lane, ...), custom_call_target="tpu_custom_call" | custom-call | bytes 10485760 | tf_op jit(solution)/shard_map/cast_pass/pallas_call | solution.py:35
  15.0 0.7 copy-done.3
  15.7 4.9 %back_product.1 = bf16[4,512,512]{2,1,0:T(8,128)(2,1)} custom-call(bf16[256,512]{1,0:T(8,128)(2,1)} %near_ref.5, bf16[256,512]{1,0:T(8,128)(2,1)} %copy-done.3, bf16[4,512,512]{2,1,0:T(8,128)(2,1)} %get-tuple-element.19.refs_8_.half_ref), custom_call_target="tpu_custom_call" | custom-call | flops 1073741824 | bytes 4194304 | tf_op jit(solution)/shard_map/back_product/pallas_call | solution.py:71
  20.6 2.7 %collective-permute-start = (bf16[256,512]{1,0:T(8,128)(2,1)S(1)}, bf16[256,512]{1,0:T(8,128)(2,1)S(1)}, u32[]{:S(2)}, u32[]{:S(2)}) collective-permute-start(bf16[256,512]{1,0:T(8,128)(2,1)S(1)} %copy-done.16), channel_id=1, source_target_pairs={{0,8},{1,9},{2,10},{3,11},{4,12},{5,13},{6,14},{7,15},{8,0},{9,1},... | collective-permute-start | bytes 786440 | tf_op jit(solution)/shard_map/ppermute | solution.py:462
  23.3 12.6 %collective-permute-done = bf16[256,512]{1,0:T(8,128)(2,1)S(1)} collective-permute-done((bf16[256,512]{1,0:T(8,128)(2,1)S(1)}, bf16[256,512]{1,0:T(8,128)(2,1)S(1)}, u32[]{:S(2)}, u32[]{:S(2)}) %collective-permute-start) | collective-permute-done | bytes 262176 | tf_op jit(solution)/shard_map/ppermute | solution.py:462
  35.9 1.6 %collective-permute-start.8 = (bf16[256,512]{1,0:T(8,128)(2,1)S(1)}, bf16[256,512]{1,0:T(8,128)(2,1)S(1)}, u32[]{:S(2)}, u32[]{:S(2)}) collective-permute-start(bf16[256,512]{1,0:T(8,128)(2,1)S(1)} %get-tuple-element.39.refs_0_), channel_id=1, source_target_pairs={{0,2},{1,3},{2,0},{3,1},{4,6},{5,7},{6,4},{7,5},{8,10},{9,11},{10,... | collective-permute-start | bytes 786440 | tf_op jit(solution)/shard_map/ppermute | solution.py:462
  37.5 0.7 collective-permute-start.4
  38.2 6.8 %weight_pass.1 = (f32[8,512,512]{2,1,0:T(8,128)}, bf16[4,512,512]{2,1,0:T(8,128)(2,1)}, bf16[4,512,512]{2,1,0:T(8,128)(2,1)}) custom-call(s32[8]{0:T(128)} %broadcast_xor_fusion.order, bf16[256,512]{1,0:T(8,128)(2,1)} %near_ref.5, bf16[256,512]{1,0:T(8,128)(2,1)} %copy-done.3, f32[8,512,512]{2,1,0:T(8,128)} %bitcast.17, ...), custom_call_target="tpu_custom_call", output_to_operand_aliasing={{0}: (4, {})} | custom-call | flops 1073741824 | bytes 12582912 | tf_op jit(solution)/shard_map/weight_pass/pallas_call | solution.py:137
  45.0 2.3 %fusion.5 = (bf16[512,512]{1,0:T(8,128)(2,1)}, bf16[512,512]{1,0:T(8,128)(2,1)S(1)}) fusion(bf16[4,512,512]{2,1,0:T(8,128)(2,1)S(1)} %collective-permute-done.18, bf16[4,512,512]{2,1,0:T(8,128)(2,1)} %get-tuple-element.27), kind=kLoop, calls=%fused_computation.12 | loop fusion | flops 2097152 | bytes 3145728 | tf_op jit(solution)/shard_map/convert_element_type | solution.py:531
  47.3 1.3 %collective-permute-start.20 = (bf16[512,512]{1,0:T(8,128)(2,1)S(1)}, bf16[512,512]{1,0:T(8,128)(2,1)S(1)}, u32[]{:S(2)}, u32[]{:S(2)}) collective-permute-start(bf16[512,512]{1,0:T(8,128)(2,1)S(1)} %get-tuple-element.37), channel_id=1, source_target_pairs={{0,4},{1,5},{2,6},{3,7},{4,0},{5,1},{6,2},{7,3},{8,12},{9,13},{10,... | collective-permute-start | bytes 1572872 | tf_op jit(solution)/shard_map/ppermute | solution.py:462
  48.7 0.6 collective-permute-start.10
  49.3 0.7 collective-permute-start.6
  50.0 0.2 collective-permute-done.1.refs_8_.refs_0_
  50.2 1.4 %collective-permute-start.12 = (bf16[256,512]{1,0:T(8,128)(2,1)S(1)}, bf16[256,512]{1,0:T(8,128)(2,1)S(1)}, u32[]{:S(2)}, u32[]{:S(2)}) collective-permute-start(bf16[256,512]{1,0:T(8,128)(2,1)S(1)} %collective-permute-done.4.refs_2_), channel_id=1, source_target_pairs={{0,2},{1,3},{2,0},{3,1},{4,6},{5,7},{6,4},{7,5},{8,10},{9,11},{10,... | collective-permute-start | bytes 786440 | tf_op jit(solution)/shard_map/ppermute | solution.py:462
  51.6 6.4 %collective-permute-done.10.refs_5_ = bf16[256,512]{1,0:T(8,128)(2,1)S(1)} collective-permute-done((bf16[256,512]{1,0:T(8,128)(2,1)S(1)}, bf16[256,512]{1,0:T(8,128)(2,1)S(1)}, u32[]{:S(2)}, u32[]{:S(2)}) %collective-permute-start.10) | collective-permute-done | bytes 262176 | tf_op jit(solution)/shard_map/ppermute | solution.py:462
  57.9 8.4 %collective-permute-done.6.refs_3_ = bf16[256,512]{1,0:T(8,128)(2,1)} collective-permute-done((bf16[256,512]{1,0:T(8,128)(2,1)S(1)}, bf16[256,512]{1,0:T(8,128)(2,1)}, u32[]{:S(2)}, u32[]{:S(2)}) %collective-permute-start.6) | collective-permute-done | bytes 262176 | tf_op jit(solution)/shard_map/ppermute | solution.py:462
  66.4 0.6 collective-permute-start.11
  67.0 0.1 copy-done.10
  67.1 0.5 collective-permute-start.14
  67.6 2.0 %fusion = bf16[512,512]{1,0:T(8,128)(2,1)} fusion(bf16[512,512]{1,0:T(8,128)(2,1)S(1)} %collective-permute-done.20, bf16[4,512,512]{2,1,0:T(8,128)(2,1)S(1)} %collective-permute-done.18, bf16[4,512,512]{2,1,0:T(8,128)(2,1)} %get-tuple-element.27), kind=kLoop, calls=%fused_computation.2 | loop fusion | flops 1572864 | bytes 2097152 | tf_op jit(solution)/shard_map/convert_element_type | solution.py:531
  69.7 0.9 collective-permute-start.19
  70.5 1.5 %collective-permute-start.21 = (bf16[512,512]{1,0:T(8,128)(2,1)}, bf16[512,512]{1,0:T(8,128)(2,1)}, u32[]{:S(2)}, u32[]{:S(2)}) collective-permute-start(bf16[512,512]{1,0:T(8,128)(2,1)} %fusion), channel_id=1, source_target_pairs={{0,2},{1,3},{2,0},{3,1},{4,6},{5,7},{6,4},{7,5},{8,10},{9,11},{10,... | collective-permute-start | bytes 1572872 | tf_op jit(solution)/shard_map/ppermute | solution.py:462
  72.1 0.7 copy-done.11
  72.8 3.8 %collective-permute-done.14.refs_7_ = bf16[256,512]{1,0:T(8,128)(2,1)} collective-permute-done((bf16[256,512]{1,0:T(8,128)(2,1)}, bf16[256,512]{1,0:T(8,128)(2,1)}, u32[]{:S(2)}, u32[]{:S(2)}) %collective-permute-start.14) | collective-permute-done | bytes 262176 | tf_op jit(solution)/shard_map/ppermute | solution.py:462
  76.6 2.3 %turn_rows.1.refs_16_ = bf16[512,512]{1,0:T(8,128)(2,1)} custom-call(bf16[256,512]{1,0:T(8,128)(2,1)} %near_ref.5, bf16[256,512]{1,0:T(8,128)(2,1)} %copy-done.3, s32[1,512]{1,0:T(1,128)} %bitcast.21), custom_call_target="tpu_custom_call" | custom-call | flops 268435456 | bytes 1048576 | tf_op jit(solution)/shard_map/turn_rows/pallas_call | solution.py:117
  78.9 9.2 %update_tiles.1 = (f32[4096,512]{1,0:T(8,128)}, f32[24,128,128]{2,1,0:T(8,128)}, f32[24,128,128]{2,1,0:T(8,128)}, bf16[24,128,128]{2,1,0:T(8,128)(2,1)}) custom-call(s32[24]{0:T(128)} %get-tuple-element.42.refs_0_.owned, s32[24]{0:T(128)} %copy-done.17, s32[24]{0:T(128)} %fusion.10.refs_2_.piece, ...), custom_call_target="tpu_custom_call", output_to_operand_aliasing={{0}: (21, {})} | custom-call | flops 402653184 | bytes 10223616 | tf_op jit(solution)/shard_map/update_tiles/pallas_call | solution.py:280
  88.1 2.1 %collective-permute-start.24 = (bf16[24,128,128]{2,1,0:T(8,128)(2,1)}, bf16[24,128,128]{2,1,0:T(8,128)(2,1)}, u32[]{:S(2)}, u32[]{:S(2)}) collective-permute-start(bf16[24,128,128]{2,1,0:T(8,128)(2,1)} %get-tuple-element.31), channel_id=1, source_target_pairs={{0,16},{16,0},{1,17},{17,1},{2,18},{18,2},{3,19},{19,3},{4,20},{20... | collective-permute-start | bytes 2359304 | tf_op jit(solution)/shard_map/ppermute | solution.py:462
  90.2 1.6 %fusion.1 = f32[512,512]{1,0:T(8,128)S(1)} fusion(bf16[512,512]{1,0:T(8,128)(2,1)} %collective-permute-done.21, bf16[512,512]{1,0:T(8,128)(2,1)} %collective-permute-done.19, bf16[4,512,512]{2,1,0:T(8,128)(2,1)S(1)} %collective-permute-done.18, bf16[4,512,512]{2,1,0:T(8,128)(2,1)} %get-tuple-element.27), kind=kLoop, calls=%fused_computation.4 | loop fusion | flops 1835008 | bytes 3145728 | tf_op jit(solution)/shard_map/add | solution.py:532
  91.9 0.1 collective-permute-start.22
  92.0 10.6 %finish_state.2 = (f32[512,512]{1,0:T(8,128)}, f32[4096,512]{1,0:T(8,128)}) custom-call(s32[24]{0:T(128)} %get-tuple-element.42.refs_0_.owned, s32[24]{0:T(128)} %copy-done.17, bf16[256,512]{1,0:T(8,128)(2,1)} %copy-done.2, bf16[256,512]{1,0:T(8,128)(2,1)} %copy-done.6, bf16[256,512]{1,0:T(8,128)(2,1)} %copy-done.5, ...), custom_call_target="tpu_custom_call" | custom-call | flops 1073741824 | bytes 16777216 | tf_op jit(solution)/shard_map/finish_state/pallas_call | solution.py:448
  102.6 5.1 %turned_product.1 = (f32[256,512]{1,0:T(8,128)}, bf16[256,512]{1,0:T(8,128)(2,1)}) custom-call(bf16[256,512]{1,0:T(8,128)(2,1)} %copy-done.9, bf16[256,512]{1,0:T(8,128)(2,1)} %copy-done.10, bf16[256,512]{1,0:T(8,128)(2,1)} %copy-done.11, bf16[256,512]{1,0:T(8,128)(2,1)} %collective-permute-done.7.refs_11_.refs_3_, bf16[256,512]{1,0:T(8,128)(2,1)} %copy-done.12, ...), custom_call_target="tpu_custom_call" | custom-call | flops 1073741824 | bytes 4194304 | tf_op jit(solution)/shard_map/turned_product/pallas_call | solution.py:406
  107.8 2.0 %collective-permute-start.17 = (bf16[256,512]{1,0:T(8,128)(2,1)}, bf16[256,512]{1,0:T(8,128)(2,1)S(1)}, u32[]{:S(2)}, u32[]{:S(2)}) collective-permute-start(bf16[256,512]{1,0:T(8,128)(2,1)} %get-tuple-element.26), channel_id=1, source_target_pairs={{0,16},{16,0},{1,17},{17,1},{2,18},{18,2},{3,19},{19,3},{4,20},{20... | collective-permute-start | bytes 786440 | tf_op jit(solution)/shard_map/ppermute | solution.py:462
  109.8 4.7 %collective-permute-done.22 = bf16[256,512]{1,0:T(8,128)(2,1)S(1)} collective-permute-done((bf16[256,512]{1,0:T(8,128)(2,1)S(1)}, bf16[256,512]{1,0:T(8,128)(2,1)S(1)}, u32[]{:S(2)}, u32[]{:S(2)}) %collective-permute-start.22) | collective-permute-done | bytes 262176 | tf_op jit(solution)/shard_map/ppermute | solution.py:462
  114.5 4.7 %collective-permute-start.23 = (bf16[256,512]{1,0:T(8,128)(2,1)S(1)}, bf16[256,512]{1,0:T(8,128)(2,1)S(1)}, u32[]{:S(2)}, u32[]{:S(2)}) collective-permute-start(bf16[256,512]{1,0:T(8,128)(2,1)S(1)} %fusion.4), channel_id=1, source_target_pairs={{0,8},{1,9},{2,10},{3,11},{4,12},{5,13},{6,14},{7,15},{8,0},{9,1},... | collective-permute-start | bytes 786440 | tf_op jit(solution)/shard_map/ppermute | solution.py:462
  119.2 8.2 %finish_state.3 = f32[4096,512]{1,0:T(8,128)} custom-call(s32[24]{0:T(128)} %get-tuple-element.42.refs_0_.owned, s32[24]{0:T(128)} %copy-done.17, f32[4096,512]{1,0:T(8,128)} %a_ref.1, f32[24,128,128]{2,1,0:T(8,128)} %get-tuple-element.30.new_ref), custom_call_target="tpu_custom_call" | custom-call | bytes 16777216 | tf_op jit(solution)/shard_map/finish_state/pallas_call | solution.py:448
  127.4 0.8 add_convert_fusion.2
  128.2 2.3 %add.81 = bf16[24,128,128]{2,1,0:T(8,128)(2,1)} add(bf16[24,128,128]{2,1,0:T(8,128)(2,1)S(1)} %copy-done.14, bf16[24,128,128]{2,1,0:T(8,128)(2,1)} %collective-permute-done.24) | non-fusion elementwise | flops 393216 | bytes 2359296 | tf_op jit(solution)/shard_map/add | solution.py:544
  130.5 0.8 fusion.3
  (69 shorter events, 0.6 us)
Async XLA Ops:
  0.6 3.1 %copy-start = (s32[64,64]{1,0:T(8,128)S(1)}, s32[64,64]{1,0:T(8,128)}, u32[]{:S(2)}) copy-start(s32[64,64]{1,0:T(8,128)} %param.14) | copy-start | bytes 49156
  0.6 14.4 %collective-permute-start.16 = (bf16[256,512]{1,0:T(8,128)(2,1)}, bf16[256,512]{1,0:T(8,128)(2,1)S(1)}, u32[]{:S(2)}, u32[]{:S(2)}) collective-permute-start(bf16[256,512]{1,0:T(8,128)(2,1)} %near_ref.5), channel_id=1, source_target_pairs={{0,16},{16,0},{1,17},{17,1},{2,18},{18,2},{3,19},{19,3},{4,20},{20... | collective-permute-start | bytes 786440 | tf_op jit(solution)/shard_map/ppermute | solution.py:462
  7.2 1.9 %copy-start.17 = (s32[24]{0:T(128)}, s32[24]{0:T(128)S(1)}, u32[]{:S(2)}) copy-start(s32[24]{0:T(128)S(1)} %get-tuple-element.35.refs_1_.row) | copy-start | bytes 292
  15.0 0.7 copy-start.3
  15.7 4.9 %copy-start.16 = (bf16[256,512]{1,0:T(8,128)(2,1)S(1)}, bf16[256,512]{1,0:T(8,128)(2,1)}, u32[]{:S(2)}) copy-start(bf16[256,512]{1,0:T(8,128)(2,1)} %param.8) | copy-start | bytes 786436
  20.6 24.4 %collective-permute-start.18 = (bf16[4,512,512]{2,1,0:T(8,128)(2,1)}, bf16[4,512,512]{2,1,0:T(8,128)(2,1)S(1)}, u32[]{:S(2)}, u32[]{:S(2)}) collective-permute-start(bf16[4,512,512]{2,1,0:T(8,128)(2,1)} %back_product.1), channel_id=1, source_target_pairs={{0,1},{1,0},{2,3},{3,2},{4,5},{5,4},{6,7},{7,6},{8,9},{9,8},{10,11... | collective-permute-start | bytes 6291464 | tf_op jit(solution)/shard_map/ppermute | solution.py:462
  20.6 15.2 %collective-permute-start = (bf16[256,512]{1,0:T(8,128)(2,1)S(1)}, bf16[256,512]{1,0:T(8,128)(2,1)S(1)}, u32[]{:S(2)}, u32[]{:S(2)}) collective-permute-start(bf16[256,512]{1,0:T(8,128)(2,1)S(1)} %copy-done.16), channel_id=1, source_target_pairs={{0,8},{1,9},{2,10},{3,11},{4,12},{5,13},{6,14},{7,15},{8,0},{9,1},... | collective-permute-start | bytes 786440 | tf_op jit(solution)/shard_map/ppermute | solution.py:462
  35.9 12.8 %copy-start.2 = (bf16[256,512]{1,0:T(8,128)(2,1)}, bf16[256,512]{1,0:T(8,128)(2,1)S(1)}, u32[]{:S(2)}) copy-start(bf16[256,512]{1,0:T(8,128)(2,1)S(1)} %get-tuple-element.39.refs_0_) | copy-start | bytes 786436
  35.9 13.3 %collective-permute-start.8 = (bf16[256,512]{1,0:T(8,128)(2,1)S(1)}, bf16[256,512]{1,0:T(8,128)(2,1)S(1)}, u32[]{:S(2)}, u32[]{:S(2)}) collective-permute-start(bf16[256,512]{1,0:T(8,128)(2,1)S(1)} %get-tuple-element.39.refs_0_), channel_id=1, source_target_pairs={{0,2},{1,3},{2,0},{3,1},{4,6},{5,7},{6,4},{7,5},{8,10},{9,11},{10,... | collective-permute-start | bytes 786440 | tf_op jit(solution)/shard_map/ppermute | solution.py:462
  37.5 12.4 %collective-permute-start.4 = (bf16[256,512]{1,0:T(8,128)(2,1)S(1)}, bf16[256,512]{1,0:T(8,128)(2,1)S(1)}, u32[]{:S(2)}, u32[]{:S(2)}) collective-permute-start(bf16[256,512]{1,0:T(8,128)(2,1)S(1)} %get-tuple-element.39.refs_0_), channel_id=1, source_target_pairs={{0,4},{1,5},{2,6},{3,7},{4,0},{5,1},{6,2},{7,3},{8,12},{9,13},{10,... | collective-permute-start | bytes 786440 | tf_op jit(solution)/shard_map/ppermute | solution.py:462
  38.2 10.5 %collective-permute-start.2 = (bf16[256,512]{1,0:T(8,128)(2,1)S(1)}, bf16[256,512]{1,0:T(8,128)(2,1)S(1)}, u32[]{:S(2)}, u32[]{:S(2)}) collective-permute-start(bf16[256,512]{1,0:T(8,128)(2,1)S(1)} %get-tuple-element.38), channel_id=1, source_target_pairs={{0,16},{16,0},{1,17},{17,1},{2,18},{18,2},{3,19},{19,3},{4,20},{20... | collective-permute-start | bytes 786440 | tf_op jit(solution)/shard_map/ppermute | solution.py:462
  47.3 19.8 %collective-permute-start.20 = (bf16[512,512]{1,0:T(8,128)(2,1)S(1)}, bf16[512,512]{1,0:T(8,128)(2,1)S(1)}, u32[]{:S(2)}, u32[]{:S(2)}) collective-permute-start(bf16[512,512]{1,0:T(8,128)(2,1)S(1)} %get-tuple-element.37), channel_id=1, source_target_pairs={{0,4},{1,5},{2,6},{3,7},{4,0},{5,1},{6,2},{7,3},{8,12},{9,13},{10,... | collective-permute-start | bytes 1572872 | tf_op jit(solution)/shard_map/ppermute | solution.py:462
  48.7 1.5 %collective-permute-start.1 = (bf16[256,512]{1,0:T(8,128)(2,1)S(1)}, bf16[256,512]{1,0:T(8,128)(2,1)S(1)}, u32[]{:S(2)}, u32[]{:S(2)}) collective-permute-start(bf16[256,512]{1,0:T(8,128)(2,1)S(1)} %get-tuple-element.39.refs_0_), channel_id=1, source_target_pairs={{0,1},{1,0},{2,3},{3,2},{4,5},{5,4},{6,7},{7,6},{8,9},{9,8},{10,11... | collective-permute-start | bytes 786440 | tf_op jit(solution)/shard_map/ppermute | solution.py:462
  48.7 30.2 %copy-start.6 = (bf16[256,512]{1,0:T(8,128)(2,1)}, bf16[256,512]{1,0:T(8,128)(2,1)S(1)}, u32[]{:S(2)}) copy-start(bf16[256,512]{1,0:T(8,128)(2,1)S(1)} %collective-permute-done.2.refs_1_) | copy-start | bytes 786436
  48.7 9.2 %collective-permute-start.10 = (bf16[256,512]{1,0:T(8,128)(2,1)S(1)}, bf16[256,512]{1,0:T(8,128)(2,1)S(1)}, u32[]{:S(2)}, u32[]{:S(2)}) collective-permute-start(bf16[256,512]{1,0:T(8,128)(2,1)S(1)} %collective-permute-done.2.refs_1_), channel_id=1, source_target_pairs={{0,2},{1,3},{2,0},{3,1},{4,6},{5,7},{6,4},{7,5},{8,10},{9,11},{10,... | collective-permute-start | bytes 786440 | tf_op jit(solution)/shard_map/ppermute | solution.py:462
  49.3 29.6 %copy-start.4 = (bf16[256,512]{1,0:T(8,128)(2,1)}, bf16[256,512]{1,0:T(8,128)(2,1)S(1)}, u32[]{:S(2)}) copy-start(bf16[256,512]{1,0:T(8,128)(2,1)S(1)} %collective-permute-done.8.refs_4_) | copy-start | bytes 786436
  49.3 17.1 %collective-permute-start.6 = (bf16[256,512]{1,0:T(8,128)(2,1)S(1)}, bf16[256,512]{1,0:T(8,128)(2,1)}, u32[]{:S(2)}, u32[]{:S(2)}) collective-permute-start(bf16[256,512]{1,0:T(8,128)(2,1)S(1)} %collective-permute-done.2.refs_1_), channel_id=1, source_target_pairs={{0,4},{1,5},{2,6},{3,7},{4,0},{5,1},{6,2},{7,3},{8,12},{9,13},{10,... | collective-permute-start | bytes 786440 | tf_op jit(solution)/shard_map/ppermute | solution.py:462
  50.0 28.9 %copy-start.5 = (bf16[256,512]{1,0:T(8,128)(2,1)}, bf16[256,512]{1,0:T(8,128)(2,1)S(1)}, u32[]{:S(2)}) copy-start(bf16[256,512]{1,0:T(8,128)(2,1)S(1)} %collective-permute-done.4.refs_2_) | copy-start | bytes 786436
  50.0 16.4 %collective-permute-start.3 = (bf16[256,512]{1,0:T(8,128)(2,1)S(1)}, bf16[256,512]{1,0:T(8,128)(2,1)S(1)}, u32[]{:S(2)}, u32[]{:S(2)}) collective-permute-start(bf16[256,512]{1,0:T(8,128)(2,1)S(1)} %collective-permute-done.2.refs_1_), channel_id=1, source_target_pairs={{0,1},{1,0},{2,3},{3,2},{4,5},{5,4},{6,7},{7,6},{8,9},{9,8},{10,11... | collective-permute-start | bytes 786440 | tf_op jit(solution)/shard_map/ppermute | solution.py:462
  50.2 16.2 %copy-start.9 = (bf16[256,512]{1,0:T(8,128)(2,1)}, bf16[256,512]{1,0:T(8,128)(2,1)S(1)}, u32[]{:S(2)}) copy-start(bf16[256,512]{1,0:T(8,128)(2,1)S(1)} %collective-permute-done.1.refs_8_.refs_0_) | copy-start | bytes 786436
  50.2 20.3 %collective-permute-start.12 = (bf16[256,512]{1,0:T(8,128)(2,1)S(1)}, bf16[256,512]{1,0:T(8,128)(2,1)S(1)}, u32[]{:S(2)}, u32[]{:S(2)}) collective-permute-start(bf16[256,512]{1,0:T(8,128)(2,1)S(1)} %collective-permute-done.4.refs_2_), channel_id=1, source_target_pairs={{0,2},{1,3},{2,0},{3,1},{4,6},{5,7},{6,4},{7,5},{8,10},{9,11},{10,... | collective-permute-start | bytes 786440 | tf_op jit(solution)/shard_map/ppermute | solution.py:462
  57.9 21.0 %copy-start.7 = (bf16[256,512]{1,0:T(8,128)(2,1)}, bf16[256,512]{1,0:T(8,128)(2,1)S(1)}, u32[]{:S(2)}) copy-start(bf16[256,512]{1,0:T(8,128)(2,1)S(1)} %collective-permute-done.10.refs_5_) | copy-start | bytes 786436
  57.9 14.1 %collective-permute-start.5 = (bf16[256,512]{1,0:T(8,128)(2,1)S(1)}, bf16[256,512]{1,0:T(8,128)(2,1)S(1)}, u32[]{:S(2)}, u32[]{:S(2)}) collective-permute-start(bf16[256,512]{1,0:T(8,128)(2,1)S(1)} %collective-permute-done.4.refs_2_), channel_id=1, source_target_pairs={{0,1},{1,0},{2,3},{3,2},{4,5},{5,4},{6,7},{7,6},{8,9},{9,8},{10,11... | collective-permute-start | bytes 786440 | tf_op jit(solution)/shard_map/ppermute | solution.py:462
  66.4 3.3 %collective-permute-start.9 = (bf16[256,512]{1,0:T(8,128)(2,1)S(1)}, bf16[256,512]{1,0:T(8,128)(2,1)S(1)}, u32[]{:S(2)}, u32[]{:S(2)}) collective-permute-start(bf16[256,512]{1,0:T(8,128)(2,1)S(1)} %collective-permute-done.8.refs_4_), channel_id=1, source_target_pairs={{0,1},{1,0},{2,3},{3,2},{4,5},{5,4},{6,7},{7,6},{8,9},{9,8},{10,11... | collective-permute-start | bytes 786440 | tf_op jit(solution)/shard_map/ppermute | solution.py:462
  66.4 0.7 copy-start.10
  66.4 5.7 %collective-permute-start.11 = (bf16[256,512]{1,0:T(8,128)(2,1)S(1)}, bf16[256,512]{1,0:T(8,128)(2,1)S(1)}, u32[]{:S(2)}, u32[]{:S(2)}) collective-permute-start(bf16[256,512]{1,0:T(8,128)(2,1)S(1)} %collective-permute-done.10.refs_5_), channel_id=1, source_target_pairs={{0,1},{1,0},{2,3},{3,2},{4,5},{5,4},{6,7},{7,6},{8,9},{9,8},{10,11... | collective-permute-start | bytes 786440 | tf_op jit(solution)/shard_map/ppermute | solution.py:462
  67.1 9.5 %collective-permute-start.14 = (bf16[256,512]{1,0:T(8,128)(2,1)}, bf16[256,512]{1,0:T(8,128)(2,1)}, u32[]{:S(2)}, u32[]{:S(2)}) collective-permute-start(bf16[256,512]{1,0:T(8,128)(2,1)} %collective-permute-done.6.refs_3_), channel_id=1, source_target_pairs={{0,2},{1,3},{2,0},{3,1},{4,6},{5,7},{6,4},{7,5},{8,10},{9,11},{10,... | collective-permute-start | bytes 786440 | tf_op jit(solution)/shard_map/ppermute | solution.py:462
  69.7 3.1 %copy-start.12 = (bf16[256,512]{1,0:T(8,128)(2,1)}, bf16[256,512]{1,0:T(8,128)(2,1)S(1)}, u32[]{:S(2)}) copy-start(bf16[256,512]{1,0:T(8,128)(2,1)S(1)} %collective-permute-done.9.refs_12_.refs_4_) | copy-start | bytes 786436
  69.7 20.6 %collective-permute-start.19 = (bf16[512,512]{1,0:T(8,128)(2,1)}, bf16[512,512]{1,0:T(8,128)(2,1)}, u32[]{:S(2)}, u32[]{:S(2)}) collective-permute-start(bf16[512,512]{1,0:T(8,128)(2,1)} %get-tuple-element.36), channel_id=1, source_target_pairs={{0,4},{1,5},{2,6},{3,7},{4,0},{5,1},{6,2},{7,3},{8,12},{9,13},{10,... | collective-permute-start | bytes 1572872 | tf_op jit(solution)/shard_map/ppermute | solution.py:462
  70.5 8.4 %copy-start.8 = (bf16[256,512]{1,0:T(8,128)(2,1)}, bf16[256,512]{1,0:T(8,128)(2,1)S(1)}, u32[]{:S(2)}) copy-start(bf16[256,512]{1,0:T(8,128)(2,1)S(1)} %collective-permute-done.12.refs_6_) | copy-start | bytes 786436
  70.5 19.7 %collective-permute-start.21 = (bf16[512,512]{1,0:T(8,128)(2,1)}, bf16[512,512]{1,0:T(8,128)(2,1)}, u32[]{:S(2)}, u32[]{:S(2)}) collective-permute-start(bf16[512,512]{1,0:T(8,128)(2,1)} %fusion), channel_id=1, source_target_pairs={{0,2},{1,3},{2,0},{3,1},{4,6},{5,7},{6,4},{7,5},{8,10},{9,11},{10,... | collective-permute-start | bytes 1572872 | tf_op jit(solution)/shard_map/ppermute | solution.py:462
  72.1 0.7 copy-start.11
  72.1 6.8 %collective-permute-start.7 = (bf16[256,512]{1,0:T(8,128)(2,1)}, bf16[256,512]{1,0:T(8,128)(2,1)}, u32[]{:S(2)}, u32[]{:S(2)}) collective-permute-start(bf16[256,512]{1,0:T(8,128)(2,1)} %collective-permute-done.6.refs_3_), channel_id=1, source_target_pairs={{0,1},{1,0},{2,3},{3,2},{4,5},{5,4},{6,7},{7,6},{8,9},{9,8},{10,11... | collective-permute-start | bytes 786440 | tf_op jit(solution)/shard_map/ppermute | solution.py:462
  72.8 3.8 %copy-start.13 = (bf16[256,512]{1,0:T(8,128)(2,1)}, bf16[256,512]{1,0:T(8,128)(2,1)S(1)}, u32[]{:S(2)}) copy-start(bf16[256,512]{1,0:T(8,128)(2,1)S(1)} %collective-permute-done.11.refs_13_.refs_5_) | copy-start | bytes 786436
  72.8 6.1 %collective-permute-start.13 = (bf16[256,512]{1,0:T(8,128)(2,1)S(1)}, bf16[256,512]{1,0:T(8,128)(2,1)}, u32[]{:S(2)}, u32[]{:S(2)}) collective-permute-start(bf16[256,512]{1,0:T(8,128)(2,1)S(1)} %collective-permute-done.12.refs_6_), channel_id=1, source_target_pairs={{0,1},{1,0},{2,3},{3,2},{4,5},{5,4},{6,7},{7,6},{8,9},{9,8},{10,11... | collective-permute-start | bytes 786440 | tf_op jit(solution)/shard_map/ppermute | solution.py:462
  76.6 2.3 %collective-permute-start.15 = (bf16[256,512]{1,0:T(8,128)(2,1)}, bf16[256,512]{1,0:T(8,128)(2,1)}, u32[]{:S(2)}, u32[]{:S(2)}) collective-permute-start(bf16[256,512]{1,0:T(8,128)(2,1)} %collective-permute-done.14.refs_7_), channel_id=1, source_target_pairs={{0,1},{1,0},{2,3},{3,2},{4,5},{5,4},{6,7},{7,6},{8,9},{9,8},{10,11... | collective-permute-start | bytes 786440 | tf_op jit(solution)/shard_map/ppermute | solution.py:462
  88.1 40.1 %collective-permute-start.24 = (bf16[24,128,128]{2,1,0:T(8,128)(2,1)}, bf16[24,128,128]{2,1,0:T(8,128)(2,1)}, u32[]{:S(2)}, u32[]{:S(2)}) collective-permute-start(bf16[24,128,128]{2,1,0:T(8,128)(2,1)} %get-tuple-element.31), channel_id=1, source_target_pairs={{0,16},{16,0},{1,17},{17,1},{2,18},{18,2},{3,19},{19,3},{4,20},{20... | collective-permute-start | bytes 2359304 | tf_op jit(solution)/shard_map/ppermute | solution.py:462
  91.9 22.6 %collective-permute-start.22 = (bf16[256,512]{1,0:T(8,128)(2,1)S(1)}, bf16[256,512]{1,0:T(8,128)(2,1)S(1)}, u32[]{:S(2)}, u32[]{:S(2)}) collective-permute-start(bf16[256,512]{1,0:T(8,128)(2,1)S(1)} %slice.69), channel_id=1, source_target_pairs={{0,16},{16,0},{1,17},{17,1},{2,18},{18,2},{3,19},{19,3},{4,20},{20... | collective-permute-start | bytes 786440 | tf_op jit(solution)/shard_map/ppermute | solution.py:462
  107.8 19.6 %collective-permute-start.17 = (bf16[256,512]{1,0:T(8,128)(2,1)}, bf16[256,512]{1,0:T(8,128)(2,1)S(1)}, u32[]{:S(2)}, u32[]{:S(2)}) collective-permute-start(bf16[256,512]{1,0:T(8,128)(2,1)} %get-tuple-element.26), channel_id=1, source_target_pairs={{0,16},{16,0},{1,17},{17,1},{2,18},{18,2},{3,19},{19,3},{4,20},{20... | collective-permute-start | bytes 786440 | tf_op jit(solution)/shard_map/ppermute | solution.py:462
  114.5 16.0 %collective-permute-start.23 = (bf16[256,512]{1,0:T(8,128)(2,1)S(1)}, bf16[256,512]{1,0:T(8,128)(2,1)S(1)}, u32[]{:S(2)}, u32[]{:S(2)}) collective-permute-start(bf16[256,512]{1,0:T(8,128)(2,1)S(1)} %fusion.4), channel_id=1, source_target_pairs={{0,8},{1,9},{2,10},{3,11},{4,12},{5,13},{6,14},{7,15},{8,0},{9,1},... | collective-permute-start | bytes 786440 | tf_op jit(solution)/shard_map/ppermute | solution.py:462
  119.2 8.2 %copy-start.15 = (f32[256,512]{1,0:T(8,128)S(1)}, f32[256,512]{1,0:T(8,128)}, u32[]{:S(2)}) copy-start(f32[256,512]{1,0:T(8,128)} %get-tuple-element.25) | copy-start | bytes 1572868
  119.2 9.0 %copy-start.14 = (bf16[24,128,128]{2,1,0:T(8,128)(2,1)S(1)}, bf16[24,128,128]{2,1,0:T(8,128)(2,1)}, u32[]{:S(2)}) copy-start(bf16[24,128,128]{2,1,0:T(8,128)(2,1)} %get-tuple-element.31) | copy-start | bytes 2359300
  127.4 3.9 %copy-start.1 = (s32[64,64]{1,0:T(8,128)S(1)}, s32[64,64]{1,0:T(8,128)}, u32[]{:S(2)}) copy-start(s32[64,64]{1,0:T(8,128)} %param.14) | copy-start | bytes 49156
where the time goes:
time: 132 us; the launch traced here: 131 us
  Pallas kernels  53.1 us (40%)
  waiting for transfers between devices  36.1 us (27%)
  starting transfers between devices  24.3 us (18%)
  other arithmetic  13.8 us (10%)
  local copies, waits for them, and re-layouts  2.91 us (2%)
    ppermute x25, waiting for transfers between devices, swap(): return lax.ppermute(a, axis, [(i, i ^ bit) for i in range(size)])  36.1 us
    ppermute x25, starting transfers between devices, swap(): return lax.ppermute(a, axis, [(i, i ^ bit) for i in range(size)])  24.3 us
    pallas_call x2, Pallas kernels, finish_state(): pl.pallas_call(kernel, out_shape=outs + [jax.ShapeDtypeStruct(a.shape, a....  18.8 us
    pallas_call x1, Pallas kernels, update_tiles(): pl.pallas_call(functools.partial(tile_kernel, slots, count, sides), out_s...  9.18 us
    pallas_call x1, Pallas kernels, weight_pass(): pl.pallas_call(weight_kernel, out_shape=(jax.ShapeDtypeStruct(blocks.shap...  6.83 us
    pallas_call x1, Pallas kernels, cast_pass(): pl.pallas_call(cast_kernel, out_shape=(jax.ShapeDtypeStruct(blocks.shape,...  6.01 us
    pallas_call x1, Pallas kernels, turned_product(): pl.pallas_call(functools.partial(turned_kernel, count), out_shape=(jax.Sh...  5.14 us
    pallas_call x1, Pallas kernels, back_product(): pl.pallas_call(back_kernel, out_shape=jax.ShapeDtypeStruct((count, rows,...  4.89 us
  transfers between devices with their start and end apart: 25, of which 6 were waited for; matrix products, arithmetic and copies ran while one was open for 11% of the time, Pallas kernels for 37%

commit v1 on v0

--- a/solution.py
+++ b/solution.py
@@ -195,7 +195,7 @@
     x_refs = refs[: count * sides]
     (
         cot_ref, w_in, m_in, v_in, w_out, m_out, v_out, fresh_ref,
-        w_buf, m_buf, v_buf, x_buf, load_sem, x_sem, store_sem,
+        w_buf, m_buf, v_buf, x_buf, load_sem, store_sem,
     ) = refs[count * sides :]
     parts = ((w_in, w_buf), (m_in, m_buf), (v_in, v_buf))
     rows = x_refs[0].shape[0]
@@ -214,24 +214,10 @@
         target = (window(w_out, i), m_out.at[i], v_out.at[i])[k]
         return pltpu.make_async_copy(parts[k][1].at[i], target, store_sem.at[k, i])
 
-    def fetch(i, n, side):
-        return pltpu.make_async_copy(
-            x_refs[n * sides + side].at[:, pl.ds(pl.multiple_of(lane[i] * TILE, TILE), TILE)],
-            x_buf.at[i, pl.ds(side * rows, rows), :],
-            x_sem.at[side, i],
-        )
-
     @pl.loop(0, slots)
     def _(i):
         @pl.when(owned[i] > 0)
         def _():
-            for n in range(count):
-
-                @pl.when(piece[i] == n)
-                def _():
-                    for side in range(sides):
-                        fetch(i, n, side).start()
-
             for k in range(3):
                 load(i, k).start()
 
@@ -239,11 +225,19 @@
     def _(i):
         @pl.when(owned[i] > 0)
         def _():
-            for side in range(sides):
-                fetch(i, 0, side).wait()
+            columns = pl.ds(pl.multiple_of(lane[i] * TILE, TILE), TILE)
+            for n in range(count):
+
+                @pl.when(piece[i] == n)
+                def _():
+                    for side in range(sides):
+                        x_buf[side * rows : (side + 1) * rows, :] = x_refs[n * sides + side][
+                            :, columns
+                        ]
+
             cot = cot_ref[:, pl.ds(pl.multiple_of(i // CAP * TILE, TILE), TILE)]
             gradient = lax.dot_general(
-                x_buf[i], cot, (((0,), (0,)), ((), ())), preferred_element_type=jnp.float32
+                x_buf[...], cot, (((0,), (0,)), ((), ())), preferred_element_type=jnp.float32
             )
             for k in range(3):
                 load(i, k).wait()
@@ -287,8 +281,8 @@
         ),
         in_specs=[smem] * 4 + [vmem] * (len(x_parts) + 1) + [hbm] * 3,
         out_specs=(hbm, hbm, hbm, vmem),
-        scratch_shapes=[buf, buf, buf, pltpu.VMEM((slots, cot.shape[0], TILE), jnp.bfloat16)]
-        + [sems, pltpu.SemaphoreType.DMA((sides, slots)), sems],
+        scratch_shapes=[buf, buf, buf, pltpu.VMEM((cot.shape[0], TILE), jnp.bfloat16)]
+        + [sems, sems],
         input_output_aliases={5 + len(x_parts): 0},
         cost_estimate=pl.CostEstimate(
             flops=2 * slots * TILE * TILE * cot.shape[0],

time: 132 us -> 132 us (level)
  no operation moved by 1% of the time
where the time goes in v1:
time: 132 us; the launch traced here: 131 us
  Pallas kernels  52.8 us (40%)
  waiting for transfers between devices  36.1 us (27%)
  starting transfers between devices  24.2 us (18%)
  other arithmetic  13.8 us (10%)
  local copies, waits for them, and re-layouts  2.91 us (2%)
    ppermute x25, waiting for transfers between devices, swap(): return lax.ppermute(a, axis, [(i, i ^ bit) for i in range(size)])  36.1 us
    ppermute x25, starting transfers between devices, swap(): return lax.ppermute(a, axis, [(i, i ^ bit) for i in range(size)])  24.2 us
    pallas_call x2, Pallas kernels, finish_state(): pl.pallas_call(kernel, out_shape=outs + [jax.ShapeDtypeStruct(a.shape, a....  18.8 us
    pallas_call x1, Pallas kernels, update_tiles(): pl.pallas_call(functools.partial(tile_kernel, slots, count, sides), out_s...  8.82 us
    pallas_call x1, Pallas kernels, weight_pass(): pl.pallas_call(weight_kernel, out_shape=(jax.ShapeDtypeStruct(blocks.shap...  6.83 us
    pallas_call x1, Pallas kernels, cast_pass(): pl.pallas_call(cast_kernel, out_shape=(jax.ShapeDtypeStruct(blocks.shape,...  6.01 us
    pallas_call x1, Pallas kernels, turned_product(): pl.pallas_call(functools.partial(turned_kernel, count), out_shape=(jax.Sh...  5.14 us
    pallas_call x1, Pallas kernels, back_product(): pl.pallas_call(back_kernel, out_shape=jax.ShapeDtypeStruct((count, rows,...  4.89 us
  transfers between devices with their start and end apart: 25, of which 6 were waited for; matrix products, arithmetic and copies ran while one was open for 11% of the time, Pallas kernels for 37%

profile of v1, /device:TPU:0, one launch (start us, length us, event | category | flops | bytes accessed | tf_op | source)
XLA Modules:
  0.0 130.9 jit_solution(9626274534688244547)
XLA Ops:
  0.6 3.0 %collective-permute-start.16 = (bf16[256,512]{1,0:T(8,128)(2,1)}, bf16[256,512]{1,0:T(8,128)(2,1)S(1)}, u32[]{:S(2)}, u32[]{:S(2)}) collective-permute-start(bf16[256,512]{1,0:T(8,128)(2,1)} %near_ref.5), channel_id=1, source_target_pairs={{0,16},{16,0},{1,17},{17,1},{2,18},{18,2},{3,19},{19,3},{4,20},{20... | collective-permute-start | bytes 786440 | tf_op jit(solution)/shard_map/ppermute | solution.py:456
  3.8 0.1 convolution_convert_fusion
  4.0 0.8 fusion.12
  4.8 0.3 select_reduce_fusion
  5.0 0.1 copy.21
  5.2 0.1 copy.22
  5.4 1.2 broadcast_xor_fusion.order
  6.6 0.6 compare_select_fusion
  7.2 0.6 fusion.10.refs_2_.piece
  7.7 1.3 subtract_select_fusion
  9.0 6.0 %cast_pass.1 = (f32[8,512,512]{2,1,0:T(8,128)}, bf16[4,512,512]{2,1,0:T(8,128)(2,1)}) custom-call(s32[8]{0:T(128)} %broadcast_xor_fusion.order, f32[8,512,512]{2,1,0:T(8,128)} %bitcast.16, s32[24]{0:T(128)} %get-tuple-element.42.refs_0_.owned, s32[24]{0:T(128)} %copy-done.17, s32[24]{0:T(128)} %fusion.10.refs_2_.piece, s32[24]{0:T(128)} %get-tuple-element.34.refs_3_.lane, ...), custom_call_target="tpu_custom_call" | custom-call | bytes 10485760 | tf_op jit(solution)/shard_map/cast_pass/pallas_call | solution.py:35
  15.0 0.7 copy-done.3
  15.7 4.9 %back_product.1 = bf16[4,512,512]{2,1,0:T(8,128)(2,1)} custom-call(bf16[256,512]{1,0:T(8,128)(2,1)} %near_ref.5, bf16[256,512]{1,0:T(8,128)(2,1)} %copy-done.3, bf16[4,512,512]{2,1,0:T(8,128)(2,1)} %get-tuple-element.19.refs_8_.half_ref), custom_call_target="tpu_custom_call" | custom-call | flops 1073741824 | bytes 4194304 | tf_op jit(solution)/shard_map/back_product/pallas_call | solution.py:71
  20.6 2.7 %collective-permute-start = (bf16[256,512]{1,0:T(8,128)(2,1)S(1)}, bf16[256,512]{1,0:T(8,128)(2,1)S(1)}, u32[]{:S(2)}, u32[]{:S(2)}) collective-permute-start(bf16[256,512]{1,0:T(8,128)(2,1)S(1)} %copy-done.16), channel_id=1, source_target_pairs={{0,8},{1,9},{2,10},{3,11},{4,12},{5,13},{6,14},{7,15},{8,0},{9,1},... | collective-permute-start | bytes 786440 | tf_op jit(solution)/shard_map/ppermute | solution.py:456
  23.3 12.6 %collective-permute-done = bf16[256,512]{1,0:T(8,128)(2,1)S(1)} collective-permute-done((bf16[256,512]{1,0:T(8,128)(2,1)S(1)}, bf16[256,512]{1,0:T(8,128)(2,1)S(1)}, u32[]{:S(2)}, u32[]{:S(2)}) %collective-permute-start) | collective-permute-done | bytes 262176 | tf_op jit(solution)/shard_map/ppermute | solution.py:456
  35.9 1.6 %collective-permute-start.8 = (bf16[256,512]{1,0:T(8,128)(2,1)S(1)}, bf16[256,512]{1,0:T(8,128)(2,1)S(1)}, u32[]{:S(2)}, u32[]{:S(2)}) collective-permute-start(bf16[256,512]{1,0:T(8,128)(2,1)S(1)} %get-tuple-element.39.refs_0_), channel_id=1, source_target_pairs={{0,2},{1,3},{2,0},{3,1},{4,6},{5,7},{6,4},{7,5},{8,10},{9,11},{10,... | collective-permute-start | bytes 786440 | tf_op jit(solution)/shard_map/ppermute | solution.py:456
  37.5 0.7 collective-permute-start.4
  38.2 6.8 %weight_pass.1 = (f32[8,512,512]{2,1,0:T(8,128)}, bf16[4,512,512]{2,1,0:T(8,128)(2,1)}, bf16[4,512,512]{2,1,0:T(8,128)(2,1)}) custom-call(s32[8]{0:T(128)} %broadcast_xor_fusion.order, bf16[256,512]{1,0:T(8,128)(2,1)} %near_ref.5, bf16[256,512]{1,0:T(8,128)(2,1)} %copy-done.3, f32[8,512,512]{2,1,0:T(8,128)} %bitcast.17, ...), custom_call_target="tpu_custom_call", output_to_operand_aliasing={{0}: (4, {})} | custom-call | flops 1073741824 | bytes 12582912 | tf_op jit(solution)/shard_map/weight_pass/pallas_call | solution.py:137
  45.0 2.3 %fusion.5 = (bf16[512,512]{1,0:T(8,128)(2,1)}, bf16[512,512]{1,0:T(8,128)(2,1)S(1)}) fusion(bf16[4,512,512]{2,1,0:T(8,128)(2,1)S(1)} %collective-permute-done.18, bf16[4,512,512]{2,1,0:T(8,128)(2,1)} %get-tuple-element.27), kind=kLoop, calls=%fused_computation.12 | loop fusion | flops 2097152 | bytes 3145728 | tf_op jit(solution)/shard_map/convert_element_type | solution.py:525
  47.3 1.3 %collective-permute-start.20 = (bf16[512,512]{1,0:T(8,128)(2,1)S(1)}, bf16[512,512]{1,0:T(8,128)(2,1)S(1)}, u32[]{:S(2)}, u32[]{:S(2)}) collective-permute-start(bf16[512,512]{1,0:T(8,128)(2,1)S(1)} %get-tuple-element.37), channel_id=1, source_target_pairs={{0,4},{1,5},{2,6},{3,7},{4,0},{5,1},{6,2},{7,3},{8,12},{9,13},{10,... | collective-permute-start | bytes 1572872 | tf_op jit(solution)/shard_map/ppermute | solution.py:456
  48.7 0.6 collective-permute-start.10
  49.3 0.7 collective-permute-start.6
  50.0 0.2 collective-permute-done.1.refs_8_.refs_0_
  50.2 1.4 %collective-permute-start.12 = (bf16[256,512]{1,0:T(8,128)(2,1)S(1)}, bf16[256,512]{1,0:T(8,128)(2,1)S(1)}, u32[]{:S(2)}, u32[]{:S(2)}) collective-permute-start(bf16[256,512]{1,0:T(8,128)(2,1)S(1)} %collective-permute-done.4.refs_2_), channel_id=1, source_target_pairs={{0,2},{1,3},{2,0},{3,1},{4,6},{5,7},{6,4},{7,5},{8,10},{9,11},{10,... | collective-permute-start | bytes 786440 | tf_op jit(solution)/shard_map/ppermute | solution.py:456
  51.6 6.4 %collective-permute-done.10.refs_5_ = bf16[256,512]{1,0:T(8,128)(2,1)S(1)} collective-permute-done((bf16[256,512]{1,0:T(8,128)(2,1)S(1)}, bf16[256,512]{1,0:T(8,128)(2,1)S(1)}, u32[]{:S(2)}, u32[]{:S(2)}) %collective-permute-start.10) | collective-permute-done | bytes 262176 | tf_op jit(solution)/shard_map/ppermute | solution.py:456
  57.9 8.4 %collective-permute-done.6.refs_3_ = bf16[256,512]{1,0:T(8,128)(2,1)} collective-permute-done((bf16[256,512]{1,0:T(8,128)(2,1)S(1)}, bf16[256,512]{1,0:T(8,128)(2,1)}, u32[]{:S(2)}, u32[]{:S(2)}) %collective-permute-start.6) | collective-permute-done | bytes 262176 | tf_op jit(solution)/shard_map/ppermute | solution.py:456
  66.4 0.6 collective-permute-start.11
  67.0 0.1 copy-done.10
  67.1 0.5 collective-permute-start.14
  67.6 2.0 %fusion = bf16[512,512]{1,0:T(8,128)(2,1)} fusion(bf16[512,512]{1,0:T(8,128)(2,1)S(1)} %collective-permute-done.20, bf16[4,512,512]{2,1,0:T(8,128)(2,1)S(1)} %collective-permute-done.18, bf16[4,512,512]{2,1,0:T(8,128)(2,1)} %get-tuple-element.27), kind=kLoop, calls=%fused_computation.2 | loop fusion | flops 1572864 | bytes 2097152 | tf_op jit(solution)/shard_map/convert_element_type | solution.py:525
  69.7 0.9 collective-permute-start.19
  70.5 1.5 %collective-permute-start.21 = (bf16[512,512]{1,0:T(8,128)(2,1)}, bf16[512,512]{1,0:T(8,128)(2,1)}, u32[]{:S(2)}, u32[]{:S(2)}) collective-permute-start(bf16[512,512]{1,0:T(8,128)(2,1)} %fusion), channel_id=1, source_target_pairs={{0,2},{1,3},{2,0},{3,1},{4,6},{5,7},{6,4},{7,5},{8,10},{9,11},{10,... | collective-permute-start | bytes 1572872 | tf_op jit(solution)/shard_map/ppermute | solution.py:456
  72.1 0.7 copy-done.11
  72.8 3.8 %collective-permute-done.14.refs_7_ = bf16[256,512]{1,0:T(8,128)(2,1)} collective-permute-done((bf16[256,512]{1,0:T(8,128)(2,1)}, bf16[256,512]{1,0:T(8,128)(2,1)}, u32[]{:S(2)}, u32[]{:S(2)}) %collective-permute-start.14) | collective-permute-done | bytes 262176 | tf_op jit(solution)/shard_map/ppermute | solution.py:456
  76.6 2.3 %turn_rows.1.refs_16_ = bf16[512,512]{1,0:T(8,128)(2,1)} custom-call(bf16[256,512]{1,0:T(8,128)(2,1)} %near_ref.5, bf16[256,512]{1,0:T(8,128)(2,1)} %copy-done.3, s32[1,512]{1,0:T(1,128)} %bitcast.21), custom_call_target="tpu_custom_call" | custom-call | flops 268435456 | bytes 1048576 | tf_op jit(solution)/shard_map/turn_rows/pallas_call | solution.py:117
  78.9 8.8 %update_tiles.1 = (f32[4096,512]{1,0:T(8,128)}, f32[24,128,128]{2,1,0:T(8,128)}, f32[24,128,128]{2,1,0:T(8,128)}, bf16[24,128,128]{2,1,0:T(8,128)(2,1)}) custom-call(s32[24]{0:T(128)} %get-tuple-element.42.refs_0_.owned, s32[24]{0:T(128)} %copy-done.17, s32[24]{0:T(128)} %fusion.10.refs_2_.piece, ...), custom_call_target="tpu_custom_call", output_to_operand_aliasing={{0}: (21, {})} | custom-call | flops 402653184 | bytes 10223616 | tf_op jit(solution)/shard_map/update_tiles/pallas_call | solution.py:274
  87.7 2.1 %collective-permute-start.24 = (bf16[24,128,128]{2,1,0:T(8,128)(2,1)}, bf16[24,128,128]{2,1,0:T(8,128)(2,1)}, u32[]{:S(2)}, u32[]{:S(2)}) collective-permute-start(bf16[24,128,128]{2,1,0:T(8,128)(2,1)} %get-tuple-element.31), channel_id=1, source_target_pairs={{0,16},{16,0},{1,17},{17,1},{2,18},{18,2},{3,19},{19,3},{4,20},{20... | collective-permute-start | bytes 2359304 | tf_op jit(solution)/shard_map/ppermute | solution.py:456
  89.8 1.6 %fusion.1 = f32[512,512]{1,0:T(8,128)S(1)} fusion(bf16[512,512]{1,0:T(8,128)(2,1)} %collective-permute-done.21, bf16[512,512]{1,0:T(8,128)(2,1)} %collective-permute-done.19, bf16[4,512,512]{2,1,0:T(8,128)(2,1)S(1)} %collective-permute-done.18, bf16[4,512,512]{2,1,0:T(8,128)(2,1)} %get-tuple-element.27), kind=kLoop, calls=%fused_computation.4 | loop fusion | flops 1835008 | bytes 3145728 | tf_op jit(solution)/shard_map/add | solution.py:526
  91.5 0.1 collective-permute-start.22
  91.6 10.6 %finish_state.2 = (f32[512,512]{1,0:T(8,128)}, f32[4096,512]{1,0:T(8,128)}) custom-call(s32[24]{0:T(128)} %get-tuple-element.42.refs_0_.owned, s32[24]{0:T(128)} %copy-done.17, bf16[256,512]{1,0:T(8,128)(2,1)} %copy-done.2, bf16[256,512]{1,0:T(8,128)(2,1)} %copy-done.6, bf16[256,512]{1,0:T(8,128)(2,1)} %copy-done.5, ...), custom_call_target="tpu_custom_call" | custom-call | flops 1073741824 | bytes 16777216 | tf_op jit(solution)/shard_map/finish_state/pallas_call | solution.py:442
  102.2 5.1 %turned_product.1 = (f32[256,512]{1,0:T(8,128)}, bf16[256,512]{1,0:T(8,128)(2,1)}) custom-call(bf16[256,512]{1,0:T(8,128)(2,1)} %copy-done.9, bf16[256,512]{1,0:T(8,128)(2,1)} %copy-done.10, bf16[256,512]{1,0:T(8,128)(2,1)} %copy-done.11, bf16[256,512]{1,0:T(8,128)(2,1)} %collective-permute-done.7.refs_11_.refs_3_, bf16[256,512]{1,0:T(8,128)(2,1)} %copy-done.12, ...), custom_call_target="tpu_custom_call" | custom-call | flops 1073741824 | bytes 4194304 | tf_op jit(solution)/shard_map/turned_product/pallas_call | solution.py:400
  107.4 2.0 %collective-permute-start.17 = (bf16[256,512]{1,0:T(8,128)(2,1)}, bf16[256,512]{1,0:T(8,128)(2,1)S(1)}, u32[]{:S(2)}, u32[]{:S(2)}) collective-permute-start(bf16[256,512]{1,0:T(8,128)(2,1)} %get-tuple-element.26), channel_id=1, source_target_pairs={{0,16},{16,0},{1,17},{17,1},{2,18},{18,2},{3,19},{19,3},{4,20},{20... | collective-permute-start | bytes 786440 | tf_op jit(solution)/shard_map/ppermute | solution.py:456
  109.4 4.7 %collective-permute-done.22 = bf16[256,512]{1,0:T(8,128)(2,1)S(1)} collective-permute-done((bf16[256,512]{1,0:T(8,128)(2,1)S(1)}, bf16[256,512]{1,0:T(8,128)(2,1)S(1)}, u32[]{:S(2)}, u32[]{:S(2)}) %collective-permute-start.22) | collective-permute-done | bytes 262176 | tf_op jit(solution)/shard_map/ppermute | solution.py:456
  114.1 4.6 %collective-permute-start.23 = (bf16[256,512]{1,0:T(8,128)(2,1)S(1)}, bf16[256,512]{1,0:T(8,128)(2,1)S(1)}, u32[]{:S(2)}, u32[]{:S(2)}) collective-permute-start(bf16[256,512]{1,0:T(8,128)(2,1)S(1)} %fusion.4), channel_id=1, source_target_pairs={{0,8},{1,9},{2,10},{3,11},{4,12},{5,13},{6,14},{7,15},{8,0},{9,1},... | collective-permute-start | bytes 786440 | tf_op jit(solution)/shard_map/ppermute | solution.py:456
  118.8 8.2 %finish_state.3 = f32[4096,512]{1,0:T(8,128)} custom-call(s32[24]{0:T(128)} %get-tuple-element.42.refs_0_.owned, s32[24]{0:T(128)} %copy-done.17, f32[4096,512]{1,0:T(8,128)} %a_ref.1, f32[24,128,128]{2,1,0:T(8,128)} %get-tuple-element.30.new_ref), custom_call_target="tpu_custom_call" | custom-call | bytes 16777216 | tf_op jit(solution)/shard_map/finish_state/pallas_call | solution.py:442
  127.0 0.8 add_convert_fusion.2
  127.8 2.3 %add.81 = bf16[24,128,128]{2,1,0:T(8,128)(2,1)} add(bf16[24,128,128]{2,1,0:T(8,128)(2,1)S(1)} %copy-done.14, bf16[24,128,128]{2,1,0:T(8,128)(2,1)} %collective-permute-done.24) | non-fusion elementwise | flops 393216 | bytes 2359296 | tf_op jit(solution)/shard_map/add | solution.py:538
  130.0 0.8 fusion.3
  (69 shorter events, 0.6 us)
Async XLA Ops:
  0.6 3.1 %copy-start = (s32[64,64]{1,0:T(8,128)S(1)}, s32[64,64]{1,0:T(8,128)}, u32[]{:S(2)}) copy-start(s32[64,64]{1,0:T(8,128)} %param.14) | copy-start | bytes 49156
  0.6 14.4 %collective-permute-start.16 = (bf16[256,512]{1,0:T(8,128)(2,1)}, bf16[256,512]{1,0:T(8,128)(2,1)S(1)}, u32[]{:S(2)}, u32[]{:S(2)}) collective-permute-start(bf16[256,512]{1,0:T(8,128)(2,1)} %near_ref.5), channel_id=1, source_target_pairs={{0,16},{16,0},{1,17},{17,1},{2,18},{18,2},{3,19},{19,3},{4,20},{20... | collective-permute-start | bytes 786440 | tf_op jit(solution)/shard_map/ppermute | solution.py:456
  7.2 1.9 %copy-start.17 = (s32[24]{0:T(128)}, s32[24]{0:T(128)S(1)}, u32[]{:S(2)}) copy-start(s32[24]{0:T(128)S(1)} %get-tuple-element.35.refs_1_.row) | copy-start | bytes 292
  15.0 0.7 copy-start.3
  15.7 4.9 %copy-start.16 = (bf16[256,512]{1,0:T(8,128)(2,1)S(1)}, bf16[256,512]{1,0:T(8,128)(2,1)}, u32[]{:S(2)}) copy-start(bf16[256,512]{1,0:T(8,128)(2,1)} %param.8) | copy-start | bytes 786436
  20.6 24.4 %collective-permute-start.18 = (bf16[4,512,512]{2,1,0:T(8,128)(2,1)}, bf16[4,512,512]{2,1,0:T(8,128)(2,1)S(1)}, u32[]{:S(2)}, u32[]{:S(2)}) collective-permute-start(bf16[4,512,512]{2,1,0:T(8,128)(2,1)} %back_product.1), channel_id=1, source_target_pairs={{0,1},{1,0},{2,3},{3,2},{4,5},{5,4},{6,7},{7,6},{8,9},{9,8},{10,11... | collective-permute-start | bytes 6291464 | tf_op jit(solution)/shard_map/ppermute | solution.py:456
  20.6 15.2 %collective-permute-start = (bf16[256,512]{1,0:T(8,128)(2,1)S(1)}, bf16[256,512]{1,0:T(8,128)(2,1)S(1)}, u32[]{:S(2)}, u32[]{:S(2)}) collective-permute-start(bf16[256,512]{1,0:T(8,128)(2,1)S(1)} %copy-done.16), channel_id=1, source_target_pairs={{0,8},{1,9},{2,10},{3,11},{4,12},{5,13},{6,14},{7,15},{8,0},{9,1},... | collective-permute-start | bytes 786440 | tf_op jit(solution)/shard_map/ppermute | solution.py:456
  35.9 12.8 %copy-start.2 = (bf16[256,512]{1,0:T(8,128)(2,1)}, bf16[256,512]{1,0:T(8,128)(2,1)S(1)}, u32[]{:S(2)}) copy-start(bf16[256,512]{1,0:T(8,128)(2,1)S(1)} %get-tuple-element.39.refs_0_) | copy-start | bytes 786436
  35.9 13.3 %collective-permute-start.8 = (bf16[256,512]{1,0:T(8,128)(2,1)S(1)}, bf16[256,512]{1,0:T(8,128)(2,1)S(1)}, u32[]{:S(2)}, u32[]{:S(2)}) collective-permute-start(bf16[256,512]{1,0:T(8,128)(2,1)S(1)} %get-tuple-element.39.refs_0_), channel_id=1, source_target_pairs={{0,2},{1,3},{2,0},{3,1},{4,6},{5,7},{6,4},{7,5},{8,10},{9,11},{10,... | collective-permute-start | bytes 786440 | tf_op jit(solution)/shard_map/ppermute | solution.py:456
  37.5 12.4 %collective-permute-start.4 = (bf16[256,512]{1,0:T(8,128)(2,1)S(1)}, bf16[256,512]{1,0:T(8,128)(2,1)S(1)}, u32[]{:S(2)}, u32[]{:S(2)}) collective-permute-start(bf16[256,512]{1,0:T(8,128)(2,1)S(1)} %get-tuple-element.39.refs_0_), channel_id=1, source_target_pairs={{0,4},{1,5},{2,6},{3,7},{4,0},{5,1},{6,2},{7,3},{8,12},{9,13},{10,... | collective-permute-start | bytes 786440 | tf_op jit(solution)/shard_map/ppermute | solution.py:456
  38.2 10.5 %collective-permute-start.2 = (bf16[256,512]{1,0:T(8,128)(2,1)S(1)}, bf16[256,512]{1,0:T(8,128)(2,1)S(1)}, u32[]{:S(2)}, u32[]{:S(2)}) collective-permute-start(bf16[256,512]{1,0:T(8,128)(2,1)S(1)} %get-tuple-element.38), channel_id=1, source_target_pairs={{0,16},{16,0},{1,17},{17,1},{2,18},{18,2},{3,19},{19,3},{4,20},{20... | collective-permute-start | bytes 786440 | tf_op jit(solution)/shard_map/ppermute | solution.py:456
  47.3 19.8 %collective-permute-start.20 = (bf16[512,512]{1,0:T(8,128)(2,1)S(1)}, bf16[512,512]{1,0:T(8,128)(2,1)S(1)}, u32[]{:S(2)}, u32[]{:S(2)}) collective-permute-start(bf16[512,512]{1,0:T(8,128)(2,1)S(1)} %get-tuple-element.37), channel_id=1, source_target_pairs={{0,4},{1,5},{2,6},{3,7},{4,0},{5,1},{6,2},{7,3},{8,12},{9,13},{10,... | collective-permute-start | bytes 1572872 | tf_op jit(solution)/shard_map/ppermute | solution.py:456
  48.7 1.5 %collective-permute-start.1 = (bf16[256,512]{1,0:T(8,128)(2,1)S(1)}, bf16[256,512]{1,0:T(8,128)(2,1)S(1)}, u32[]{:S(2)}, u32[]{:S(2)}) collective-permute-start(bf16[256,512]{1,0:T(8,128)(2,1)S(1)} %get-tuple-element.39.refs_0_), channel_id=1, source_target_pairs={{0,1},{1,0},{2,3},{3,2},{4,5},{5,4},{6,7},{7,6},{8,9},{9,8},{10,11... | collective-permute-start | bytes 786440 | tf_op jit(solution)/shard_map/ppermute | solution.py:456
  48.7 30.2 %copy-start.6 = (bf16[256,512]{1,0:T(8,128)(2,1)}, bf16[256,512]{1,0:T(8,128)(2,1)S(1)}, u32[]{:S(2)}) copy-start(bf16[256,512]{1,0:T(8,128)(2,1)S(1)} %collective-permute-done.2.refs_1_) | copy-start | bytes 786436
  48.7 9.2 %collective-permute-start.10 = (bf16[256,512]{1,0:T(8,128)(2,1)S(1)}, bf16[256,512]{1,0:T(8,128)(2,1)S(1)}, u32[]{:S(2)}, u32[]{:S(2)}) collective-permute-start(bf16[256,512]{1,0:T(8,128)(2,1)S(1)} %collective-permute-done.2.refs_1_), channel_id=1, source_target_pairs={{0,2},{1,3},{2,0},{3,1},{4,6},{5,7},{6,4},{7,5},{8,10},{9,11},{10,... | collective-permute-start | bytes 786440 | tf_op jit(solution)/shard_map/ppermute | solution.py:456
  49.3 29.6 %copy-start.4 = (bf16[256,512]{1,0:T(8,128)(2,1)}, bf16[256,512]{1,0:T(8,128)(2,1)S(1)}, u32[]{:S(2)}) copy-start(bf16[256,512]{1,0:T(8,128)(2,1)S(1)} %collective-permute-done.8.refs_4_) | copy-start | bytes 786436
  49.3 17.1 %collective-permute-start.6 = (bf16[256,512]{1,0:T(8,128)(2,1)S(1)}, bf16[256,512]{1,0:T(8,128)(2,1)}, u32[]{:S(2)}, u32[]{:S(2)}) collective-permute-start(bf16[256,512]{1,0:T(8,128)(2,1)S(1)} %collective-permute-done.2.refs_1_), channel_id=1, source_target_pairs={{0,4},{1,5},{2,6},{3,7},{4,0},{5,1},{6,2},{7,3},{8,12},{9,13},{10,... | collective-permute-start | bytes 786440 | tf_op jit(solution)/shard_map/ppermute | solution.py:456
  50.0 28.9 %copy-start.5 = (bf16[256,512]{1,0:T(8,128)(2,1)}, bf16[256,512]{1,0:T(8,128)(2,1)S(1)}, u32[]{:S(2)}) copy-start(bf16[256,512]{1,0:T(8,128)(2,1)S(1)} %collective-permute-done.4.refs_2_) | copy-start | bytes 786436
  50.0 16.4 %collective-permute-start.3 = (bf16[256,512]{1,0:T(8,128)(2,1)S(1)}, bf16[256,512]{1,0:T(8,128)(2,1)S(1)}, u32[]{:S(2)}, u32[]{:S(2)}) collective-permute-start(bf16[256,512]{1,0:T(8,128)(2,1)S(1)} %collective-permute-done.2.refs_1_), channel_id=1, source_target_pairs={{0,1},{1,0},{2,3},{3,2},{4,5},{5,4},{6,7},{7,6},{8,9},{9,8},{10,11... | collective-permute-start | bytes 786440 | tf_op jit(solution)/shard_map/ppermute | solution.py:456
  50.2 16.2 %copy-start.9 = (bf16[256,512]{1,0:T(8,128)(2,1)}, bf16[256,512]{1,0:T(8,128)(2,1)S(1)}, u32[]{:S(2)}) copy-start(bf16[256,512]{1,0:T(8,128)(2,1)S(1)} %collective-permute-done.1.refs_8_.refs_0_) | copy-start | bytes 786436
  50.2 20.3 %collective-permute-start.12 = (bf16[256,512]{1,0:T(8,128)(2,1)S(1)}, bf16[256,512]{1,0:T(8,128)(2,1)S(1)}, u32[]{:S(2)}, u32[]{:S(2)}) collective-permute-start(bf16[256,512]{1,0:T(8,128)(2,1)S(1)} %collective-permute-done.4.refs_2_), channel_id=1, source_target_pairs={{0,2},{1,3},{2,0},{3,1},{4,6},{5,7},{6,4},{7,5},{8,10},{9,11},{10,... | collective-permute-start | bytes 786440 | tf_op jit(solution)/shard_map/ppermute | solution.py:456
  57.9 21.0 %copy-start.7 = (bf16[256,512]{1,0:T(8,128)(2,1)}, bf16[256,512]{1,0:T(8,128)(2,1)S(1)}, u32[]{:S(2)}) copy-start(bf16[256,512]{1,0:T(8,128)(2,1)S(1)} %collective-permute-done.10.refs_5_) | copy-start | bytes 786436
  57.9 14.1 %collective-permute-start.5 = (bf16[256,512]{1,0:T(8,128)(2,1)S(1)}, bf16[256,512]{1,0:T(8,128)(2,1)S(1)}, u32[]{:S(2)}, u32[]{:S(2)}) collective-permute-start(bf16[256,512]{1,0:T(8,128)(2,1)S(1)} %collective-permute-done.4.refs_2_), channel_id=1, source_target_pairs={{0,1},{1,0},{2,3},{3,2},{4,5},{5,4},{6,7},{7,6},{8,9},{9,8},{10,11... | collective-permute-start | bytes 786440 | tf_op jit(solution)/shard_map/ppermute | solution.py:456
  66.4 3.3 %collective-permute-start.9 = (bf16[256,512]{1,0:T(8,128)(2,1)S(1)}, bf16[256,512]{1,0:T(8,128)(2,1)S(1)}, u32[]{:S(2)}, u32[]{:S(2)}) collective-permute-start(bf16[256,512]{1,0:T(8,128)(2,1)S(1)} %collective-permute-done.8.refs_4_), channel_id=1, source_target_pairs={{0,1},{1,0},{2,3},{3,2},{4,5},{5,4},{6,7},{7,6},{8,9},{9,8},{10,11... | collective-permute-start | bytes 786440 | tf_op jit(solution)/shard_map/ppermute | solution.py:456
  66.4 0.7 copy-start.10
  66.4 5.7 %collective-permute-start.11 = (bf16[256,512]{1,0:T(8,128)(2,1)S(1)}, bf16[256,512]{1,0:T(8,128)(2,1)S(1)}, u32[]{:S(2)}, u32[]{:S(2)}) collective-permute-start(bf16[256,512]{1,0:T(8,128)(2,1)S(1)} %collective-permute-done.10.refs_5_), channel_id=1, source_target_pairs={{0,1},{1,0},{2,3},{3,2},{4,5},{5,4},{6,7},{7,6},{8,9},{9,8},{10,11... | collective-permute-start | bytes 786440 | tf_op jit(solution)/shard_map/ppermute | solution.py:456
  67.1 9.5 %collective-permute-start.14 = (bf16[256,512]{1,0:T(8,128)(2,1)}, bf16[256,512]{1,0:T(8,128)(2,1)}, u32[]{:S(2)}, u32[]{:S(2)}) collective-permute-start(bf16[256,512]{1,0:T(8,128)(2,1)} %collective-permute-done.6.refs_3_), channel_id=1, source_target_pairs={{0,2},{1,3},{2,0},{3,1},{4,6},{5,7},{6,4},{7,5},{8,10},{9,11},{10,... | collective-permute-start | bytes 786440 | tf_op jit(solution)/shard_map/ppermute | solution.py:456
  69.7 3.1 %copy-start.12 = (bf16[256,512]{1,0:T(8,128)(2,1)}, bf16[256,512]{1,0:T(8,128)(2,1)S(1)}, u32[]{:S(2)}) copy-start(bf16[256,512]{1,0:T(8,128)(2,1)S(1)} %collective-permute-done.9.refs_12_.refs_4_) | copy-start | bytes 786436
  69.7 20.2 %collective-permute-start.19 = (bf16[512,512]{1,0:T(8,128)(2,1)}, bf16[512,512]{1,0:T(8,128)(2,1)}, u32[]{:S(2)}, u32[]{:S(2)}) collective-permute-start(bf16[512,512]{1,0:T(8,128)(2,1)} %get-tuple-element.36), channel_id=1, source_target_pairs={{0,4},{1,5},{2,6},{3,7},{4,0},{5,1},{6,2},{7,3},{8,12},{9,13},{10,... | collective-permute-start | bytes 1572872 | tf_op jit(solution)/shard_map/ppermute | solution.py:456
  70.5 8.4 %copy-start.8 = (bf16[256,512]{1,0:T(8,128)(2,1)}, bf16[256,512]{1,0:T(8,128)(2,1)S(1)}, u32[]{:S(2)}) copy-start(bf16[256,512]{1,0:T(8,128)(2,1)S(1)} %collective-permute-done.12.refs_6_) | copy-start | bytes 786436
  70.5 19.3 %collective-permute-start.21 = (bf16[512,512]{1,0:T(8,128)(2,1)}, bf16[512,512]{1,0:T(8,128)(2,1)}, u32[]{:S(2)}, u32[]{:S(2)}) collective-permute-start(bf16[512,512]{1,0:T(8,128)(2,1)} %fusion), channel_id=1, source_target_pairs={{0,2},{1,3},{2,0},{3,1},{4,6},{5,7},{6,4},{7,5},{8,10},{9,11},{10,... | collective-permute-start | bytes 1572872 | tf_op jit(solution)/shard_map/ppermute | solution.py:456
  72.1 0.7 copy-start.11
  72.1 6.8 %collective-permute-start.7 = (bf16[256,512]{1,0:T(8,128)(2,1)}, bf16[256,512]{1,0:T(8,128)(2,1)}, u32[]{:S(2)}, u32[]{:S(2)}) collective-permute-start(bf16[256,512]{1,0:T(8,128)(2,1)} %collective-permute-done.6.refs_3_), channel_id=1, source_target_pairs={{0,1},{1,0},{2,3},{3,2},{4,5},{5,4},{6,7},{7,6},{8,9},{9,8},{10,11... | collective-permute-start | bytes 786440 | tf_op jit(solution)/shard_map/ppermute | solution.py:456
  72.8 3.8 %copy-start.13 = (bf16[256,512]{1,0:T(8,128)(2,1)}, bf16[256,512]{1,0:T(8,128)(2,1)S(1)}, u32[]{:S(2)}) copy-start(bf16[256,512]{1,0:T(8,128)(2,1)S(1)} %collective-permute-done.11.refs_13_.refs_5_) | copy-start | bytes 786436
  72.8 6.1 %collective-permute-start.13 = (bf16[256,512]{1,0:T(8,128)(2,1)S(1)}, bf16[256,512]{1,0:T(8,128)(2,1)}, u32[]{:S(2)}, u32[]{:S(2)}) collective-permute-start(bf16[256,512]{1,0:T(8,128)(2,1)S(1)} %collective-permute-done.12.refs_6_), channel_id=1, source_target_pairs={{0,1},{1,0},{2,3},{3,2},{4,5},{5,4},{6,7},{7,6},{8,9},{9,8},{10,11... | collective-permute-start | bytes 786440 | tf_op jit(solution)/shard_map/ppermute | solution.py:456
  76.6 2.3 %collective-permute-start.15 = (bf16[256,512]{1,0:T(8,128)(2,1)}, bf16[256,512]{1,0:T(8,128)(2,1)}, u32[]{:S(2)}, u32[]{:S(2)}) collective-permute-start(bf16[256,512]{1,0:T(8,128)(2,1)} %collective-permute-done.14.refs_7_), channel_id=1, source_target_pairs={{0,1},{1,0},{2,3},{3,2},{4,5},{5,4},{6,7},{7,6},{8,9},{9,8},{10,11... | collective-permute-start | bytes 786440 | tf_op jit(solution)/shard_map/ppermute | solution.py:456
  87.7 40.0 %collective-permute-start.24 = (bf16[24,128,128]{2,1,0:T(8,128)(2,1)}, bf16[24,128,128]{2,1,0:T(8,128)(2,1)}, u32[]{:S(2)}, u32[]{:S(2)}) collective-permute-start(bf16[24,128,128]{2,1,0:T(8,128)(2,1)} %get-tuple-element.31), channel_id=1, source_target_pairs={{0,16},{16,0},{1,17},{17,1},{2,18},{18,2},{3,19},{19,3},{4,20},{20... | collective-permute-start | bytes 2359304 | tf_op jit(solution)/shard_map/ppermute | solution.py:456
  91.5 22.6 %collective-permute-start.22 = (bf16[256,512]{1,0:T(8,128)(2,1)S(1)}, bf16[256,512]{1,0:T(8,128)(2,1)S(1)}, u32[]{:S(2)}, u32[]{:S(2)}) collective-permute-start(bf16[256,512]{1,0:T(8,128)(2,1)S(1)} %slice.69), channel_id=1, source_target_pairs={{0,16},{16,0},{1,17},{17,1},{2,18},{18,2},{3,19},{19,3},{4,20},{20... | collective-permute-start | bytes 786440 | tf_op jit(solution)/shard_map/ppermute | solution.py:456
  107.4 19.6 %collective-permute-start.17 = (bf16[256,512]{1,0:T(8,128)(2,1)}, bf16[256,512]{1,0:T(8,128)(2,1)S(1)}, u32[]{:S(2)}, u32[]{:S(2)}) collective-permute-start(bf16[256,512]{1,0:T(8,128)(2,1)} %get-tuple-element.26), channel_id=1, source_target_pairs={{0,16},{16,0},{1,17},{17,1},{2,18},{18,2},{3,19},{19,3},{4,20},{20... | collective-permute-start | bytes 786440 | tf_op jit(solution)/shard_map/ppermute | solution.py:456
  114.1 15.9 %collective-permute-start.23 = (bf16[256,512]{1,0:T(8,128)(2,1)S(1)}, bf16[256,512]{1,0:T(8,128)(2,1)S(1)}, u32[]{:S(2)}, u32[]{:S(2)}) collective-permute-start(bf16[256,512]{1,0:T(8,128)(2,1)S(1)} %fusion.4), channel_id=1, source_target_pairs={{0,8},{1,9},{2,10},{3,11},{4,12},{5,13},{6,14},{7,15},{8,0},{9,1},... | collective-permute-start | bytes 786440 | tf_op jit(solution)/shard_map/ppermute | solution.py:456
  118.8 8.2 %copy-start.15 = (f32[256,512]{1,0:T(8,128)S(1)}, f32[256,512]{1,0:T(8,128)}, u32[]{:S(2)}) copy-start(f32[256,512]{1,0:T(8,128)} %get-tuple-element.25) | copy-start | bytes 1572868
  118.8 9.0 %copy-start.14 = (bf16[24,128,128]{2,1,0:T(8,128)(2,1)S(1)}, bf16[24,128,128]{2,1,0:T(8,128)(2,1)}, u32[]{:S(2)}) copy-start(bf16[24,128,128]{2,1,0:T(8,128)(2,1)} %get-tuple-element.31) | copy-start | bytes 2359300
  127.0 3.9 %copy-start.1 = (s32[64,64]{1,0:T(8,128)S(1)}, s32[64,64]{1,0:T(8,128)}, u32[]{:S(2)}) copy-start(s32[64,64]{1,0:T(8,128)} %param.14) | copy-start | bytes 49156

commit v2 on v1

--- a/solution.py
+++ b/solution.py
@@ -20,35 +20,84 @@
 bias_two = 1.0 - 0.999**10
 
 
-def cast_kernel(order, w_ref, *refs):
-    copy_ref, half_ref = refs[-2:]
-    w = w_ref[...]
-    copy_ref[...] = w
-    half_ref[...] = w.astype(jnp.bfloat16)
-
-
-def cast_pass(blocks, order, first=0, after=()):
-    count = order.shape[0] - first
+def stream_kernel(count, first, order, *refs):
+    products = len(refs) > 10
+    if products:
+        near_ref, other_ref, w_ref, _, copy_ref, half_ref, out_ref, *rest = refs
+        w_buf, half_buf, out_buf, load_sem, copy_sem, half_sem, out_sem = rest
+        cot = jnp.concatenate([near_ref[...], other_ref[...]], axis=0)
+    else:
+        w_ref, copy_ref, half_ref, w_buf, half_buf, load_sem, copy_sem, half_sem = refs
+
+    def load(n):
+        return pltpu.make_async_copy(w_ref.at[order[first + n]], w_buf.at[n], load_sem.at[n])
+
+    def stores(n):
+        put = pltpu.make_async_copy
+        some = [
+            put(w_buf.at[n], copy_ref.at[order[first + n]], copy_sem.at[n]),
+            put(half_buf.at[n], half_ref.at[n], half_sem.at[n]),
+        ]
+        return some + ([put(out_buf.at[n], out_ref.at[n], out_sem.at[n])] if products else [])
+
+    for n in range(count):
+        load(n).start()
+    for n in range(count):
+        load(n).wait()
+        half = w_buf[n].astype(jnp.bfloat16)
+        half_buf[n] = half
+        copies = stores(n)
+        copies[0].start()
+        copies[1].start()
+        if products:
+            out_buf[n] = lax.dot_general(
+                cot, half, (((1,), (1,)), ((), ())), preferred_element_type=jnp.float32
+            ).astype(out_buf.dtype)
+            copies[2].start()
+    for n in range(count):
+        for copy in stores(n):
+            copy.wait()
+
+
+def stream_pass(blocks, order, count, first=0, pair=(), copied=None, after=()):
     _, depth, width = blocks.shape
-    take = pl.BlockSpec((1, depth, width), lambda i, order: (order[i + first], 0, 0))
-    put = pl.BlockSpec((1, depth, width), lambda i, order: (i, 0, 0))
+    smem = pl.BlockSpec(memory_space=pltpu.SMEM)
+    vmem = pl.BlockSpec(memory_space=pltpu.VMEM)
+    hbm = pl.BlockSpec(memory_space=pl.ANY)
+    outs = [
+        jax.ShapeDtypeStruct(blocks.shape, jnp.float32),
+        jax.ShapeDtypeStruct((count, depth, width), jnp.bfloat16),
+    ]
+    scratch = [
+        pltpu.VMEM((count, depth, width), jnp.float32),
+        pltpu.VMEM((count, depth, width), jnp.bfloat16),
+    ]
+    more, rows = [], 0
+    if pair:
+        rows = pair[0].shape[0] + pair[1].shape[0]
+        outs.append(jax.ShapeDtypeStruct((count, rows, depth), jnp.bfloat16))
+        scratch.append(pltpu.VMEM((count, rows, depth), jnp.bfloat16))
+        more = [copied]
+    kept = len(pair) + 1 + len(more)
+    body = functools.partial(stream_kernel, count, first)
+
+    def kernel(order_ref, *refs):
+        body(order_ref, *refs[:kept], *refs[kept + len(after) :])
+
     return pl.pallas_call(
-        cast_kernel,
-        out_shape=(
-            jax.ShapeDtypeStruct(blocks.shape, jnp.float32),
-            jax.ShapeDtypeStruct((count, depth, width), jnp.bfloat16),
-        ),
-        grid_spec=pltpu.PrefetchScalarGridSpec(
-            num_scalar_prefetch=1,
-            grid=(count,),
-            in_specs=[take] + [pl.BlockSpec(memory_space=pl.ANY)] * len(after),
-            out_specs=(take, put),
-        ),
+        kernel,
+        out_shape=outs,
+        in_specs=[smem] + [vmem] * len(pair) + [hbm] * (1 + len(more) + len(after)),
+        out_specs=[hbm] * len(outs),
+        scratch_shapes=scratch + [pltpu.SemaphoreType.DMA((count,))] * (len(outs) + 1),
+        input_output_aliases={1 + len(pair) + 1: 0} if more else {},
         cost_estimate=pl.CostEstimate(
-            flops=0, bytes_accessed=10 * count * depth * width, transcendentals=0
-        ),
-        name="cast_pass",
-    )(order, blocks, *after)
+            flops=2 * count * rows * width * depth,
+            bytes_accessed=count * depth * (10 * width + 2 * rows),
+            transcendentals=0,
+        ),
+        name="stream_pass",
+    )(order, *pair, blocks, *more, *after)
 
 
 def back_kernel(near_ref, other_ref, half_ref, out_ref, cot_ref):
@@ -84,25 +133,6 @@
     )(near, other, half)
 
 
-def weight_kernel(
-    order, near_ref, other_ref, w_ref, _, copy_ref, half_ref, out_ref, cot_ref
-):
-    rows = near_ref.shape[0]
-
-    @pl.when(pl.program_id(0) == 0)
-    def _():
-        cot_ref[:rows, :] = near_ref[...]
-        cot_ref[rows:, :] = other_ref[...]
-
-    w = w_ref[0]
-    copy_ref[0] = w
-    half = w.astype(jnp.bfloat16)
-    half_ref[0] = half
-    out_ref[0] = lax.dot_general(
-        cot_ref[...], half, (((1,), (1,)), ((), ())), preferred_element_type=jnp.float32
-    ).astype(out_ref.dtype)
-
-
 def turn_kernel(near_ref, other_ref, turn_ref, out_ref):
     rows = near_ref.shape[0]
     place = lax.broadcasted_iota(jnp.int32, (2 * rows, 2 * rows), 0)
@@ -124,38 +154,6 @@
         ),
         name="turn_rows",
     )(near, other, turn)
-
-
-def weight_pass(near, other, blocks, order, count, copied):
-    width = near.shape[1]
-    rows = near.shape[0] + other.shape[0]
-    depth = blocks.shape[1]
-    vmem = pl.BlockSpec(memory_space=pltpu.VMEM)
-    take = pl.BlockSpec((1, depth, width), lambda i, order: (order[i], 0, 0))
-    put = pl.BlockSpec((1, depth, width), lambda i, order: (i, 0, 0))
-    out = pl.BlockSpec((1, rows, depth), lambda i, order: (i, 0, 0))
-    return pl.pallas_call(
-        weight_kernel,
-        out_shape=(
-            jax.ShapeDtypeStruct(blocks.shape, jnp.float32),
-            jax.ShapeDtypeStruct((count, depth, width), jnp.bfloat16),
-            jax.ShapeDtypeStruct((count, rows, depth), jnp.bfloat16),
-        ),
-        grid_spec=pltpu.PrefetchScalarGridSpec(
-            num_scalar_prefetch=1,
-            grid=(count,),
-            in_specs=[vmem, vmem, take, pl.BlockSpec(memory_space=pl.ANY)],
-            out_specs=(take, put, out),
-            scratch_shapes=[pltpu.VMEM((rows, width), jnp.bfloat16)],
-        ),
-        input_output_aliases={4: 0},
-        cost_estimate=pl.CostEstimate(
-            flops=2 * count * rows * width * depth,
-            bytes_accessed=count * depth * (10 * width + 2 * rows),
-            transcendentals=0,
-        ),
-        name="weight_pass",
-    )(order, near, other, blocks, copied)
 
 
 def forward_kernel(x_ref, w_ref, out_ref):
@@ -503,7 +501,7 @@
 
     cot_other = swap(cotangent, "group", groups, 1)
     far = swap(rollout_rows, "shard", shard_count, half_count)
-    w_copy, half_high = cast_pass(blocks, order, low, (owned, row, piece, lane, turn))
+    w_copy, half_high = stream_pass(blocks, order, low, low, after=(owned, row, piece, lane, turn))
     sent = back_product(cotangent, cot_other, half_high)
     got = swap(sent, "shard", shard_count, bits[-1])
     keep = jnp.where(in_half, rollout_rows, far)
@@ -514,7 +512,9 @@
         for part in held:
             x_parts.append(swap(part, "shard", shard_count, bit))
 
-    w_copy, half_low, kept = weight_pass(cotangent, cot_other, blocks, order, low, w_copy)
+    w_copy, half_low, kept = stream_pass(
+        blocks, order, low, 0, (cotangent, cot_other), w_copy
+    )
     cot_turned = turn_rows(cotangent, cot_other, turn)
     terms = {
         o: kept[n].astype(jnp.float32) + got[n].astype(jnp.float32)
@@ -558,7 +558,7 @@
     per_group = shard_count // groups
     row_total = groups * row_count
     order = jnp.arange(per_group, dtype=jnp.int32)
-    w_copy, half = cast_pass(w_master.reshape(per_group, -1, width), order)
+    w_copy, half = stream_pass(w_master.reshape(per_group, -1, width), order, per_group)
     x_cols = lax.all_gather(rollout_rows, "group", axis=0, tiled=True)
     x_full = lax.all_gather(x_cols, "shard", axis=0)
     x_all = lax.dynamic_slice_in_dim(x_full, group_at * per_group, per_group, 0)

time: 132 us -> 129 us (0.977)
  Pallas kernels: 52.8 us -> 50.3 us
    pallas_call x2, Pallas kernels: 12.8 us -> 10.3 us  [stream_pass(): pl.pallas_call(kernel, out_shape=outs, in_specs=[smem] + [vmem] * len(pai...]
  transfers between devices with their start and end apart: 25 -> 25, of which waited for: 6 -> 6; matrix products, arithmetic and copies ran while one was open for 11% -> 11% of each run, Pallas kernels for 37% -> 35%
where the time goes in v2:
time: 129 us; the launch traced here: 128 us
  Pallas kernels  50.3 us (39%)
  waiting for transfers between devices  36.1 us (28%)
  starting transfers between devices  24.2 us (19%)
  other arithmetic  13.8 us (11%)
  local copies, waits for them, and re-layouts  2.91 us (2%)
    ppermute x25, waiting for transfers between devices, swap(): return lax.ppermute(a, axis, [(i, i ^ bit) for i in range(size)])  36.1 us
    ppermute x25, starting transfers between devices, swap(): return lax.ppermute(a, axis, [(i, i ^ bit) for i in range(size)])  24.2 us
    pallas_call x2, Pallas kernels, finish_state(): pl.pallas_call(kernel, out_shape=outs + [jax.ShapeDtypeStruct(a.shape, a....  18.8 us
    pallas_call x2, Pallas kernels, stream_pass(): pl.pallas_call(kernel, out_shape=outs, in_specs=[smem] + [vmem] * len(pai...  10.3 us
    pallas_call x1, Pallas kernels, update_tiles(): pl.pallas_call(functools.partial(tile_kernel, slots, count, sides), out_s...  8.82 us
    pallas_call x1, Pallas kernels, turned_product(): pl.pallas_call(functools.partial(turned_kernel, count), out_shape=(jax.Sh...  5.14 us
    pallas_call x1, Pallas kernels, back_product(): pl.pallas_call(back_kernel, out_shape=jax.ShapeDtypeStruct((count, rows,...  4.89 us
    convert_element_type x2, other arithmetic, pair_shards(): term = swap(terms.pop(o).astype(jnp.bfloat16), 'shard', shard_count, bit)  4.34 us
  transfers between devices with their start and end apart: 25, of which 6 were waited for; matrix products, arithmetic and copies ran while one was open for 11% of the time, Pallas kernels for 35%

profile of v2, /device:TPU:0, one launch (start us, length us, event | category | flops | bytes accessed | tf_op | source)
XLA Modules:
  0.0 128.4 jit_solution(1640644310990922841)
XLA Ops:
  0.6 3.0 %collective-permute-start.16 = (bf16[256,512]{1,0:T(8,128)(2,1)}, bf16[256,512]{1,0:T(8,128)(2,1)S(1)}, u32[]{:S(2)}, u32[]{:S(2)}) collective-permute-start(bf16[256,512]{1,0:T(8,128)(2,1)} %near_ref.3), channel_id=1, source_target_pairs={{0,16},{16,0},{1,17},{17,1},{2,18},{18,2},{3,19},{19,3},{4,20},{20... | collective-permute-start | bytes 786440 | tf_op jit(solution)/shard_map/ppermute | solution.py:454
  3.8 0.1 convolution_convert_fusion
  4.0 0.8 fusion.12
  4.8 0.3 select_reduce_fusion
  5.0 0.1 copy.21
  5.2 0.1 copy.22
  5.4 1.2 broadcast_xor_fusion.order_ref
  6.6 0.6 compare_select_fusion
  7.2 0.6 fusion.10.refs_3_.piece
  7.7 1.3 subtract_select_fusion
  9.0 4.6 %stream_pass.2 = (f32[8,512,512]{2,1,0:T(8,128)}, bf16[4,512,512]{2,1,0:T(8,128)(2,1)}) custom-call(s32[8]{0:T(128)} %broadcast_xor_fusion.order_ref, f32[8,512,512]{2,1,0:T(8,128)} %bitcast.16, s32[24]{0:T(128)} %get-tuple-element.42.refs_1_.owned, s32[24]{0:T(128)} %copy-done.17, s32[24]{0:T(128)} %fusion.10.refs_3_.piece, ...), custom_call_target="tpu_custom_call" | custom-call | bytes 10485760 | tf_op jit(solution)/shard_map/stream_pass/pallas_call | solution.py:87
  13.7 0.7 copy-done.3
  14.4 4.9 %back_product.1 = bf16[4,512,512]{2,1,0:T(8,128)(2,1)} custom-call(bf16[256,512]{1,0:T(8,128)(2,1)} %near_ref.3, bf16[256,512]{1,0:T(8,128)(2,1)} %copy-done.3, bf16[4,512,512]{2,1,0:T(8,128)(2,1)} %get-tuple-element.19.refs_8_.half_ref), custom_call_target="tpu_custom_call" | custom-call | flops 1073741824 | bytes 4194304 | tf_op jit(solution)/shard_map/back_product/pallas_call | solution.py:120
  19.3 2.7 %collective-permute-start = (bf16[256,512]{1,0:T(8,128)(2,1)S(1)}, bf16[256,512]{1,0:T(8,128)(2,1)S(1)}, u32[]{:S(2)}, u32[]{:S(2)}) collective-permute-start(bf16[256,512]{1,0:T(8,128)(2,1)S(1)} %copy-done.16), channel_id=1, source_target_pairs={{0,8},{1,9},{2,10},{3,11},{4,12},{5,13},{6,14},{7,15},{8,0},{9,1},... | collective-permute-start | bytes 786440 | tf_op jit(solution)/shard_map/ppermute | solution.py:454
  21.9 12.6 %collective-permute-done = bf16[256,512]{1,0:T(8,128)(2,1)S(1)} collective-permute-done((bf16[256,512]{1,0:T(8,128)(2,1)S(1)}, bf16[256,512]{1,0:T(8,128)(2,1)S(1)}, u32[]{:S(2)}, u32[]{:S(2)}) %collective-permute-start) | collective-permute-done | bytes 262176 | tf_op jit(solution)/shard_map/ppermute | solution.py:454
  34.6 1.6 %collective-permute-start.8 = (bf16[256,512]{1,0:T(8,128)(2,1)S(1)}, bf16[256,512]{1,0:T(8,128)(2,1)S(1)}, u32[]{:S(2)}, u32[]{:S(2)}) collective-permute-start(bf16[256,512]{1,0:T(8,128)(2,1)S(1)} %get-tuple-element.39.refs_0_), channel_id=1, source_target_pairs={{0,2},{1,3},{2,0},{3,1},{4,6},{5,7},{6,4},{7,5},{8,10},{9,11},{10,... | collective-permute-start | bytes 786440 | tf_op jit(solution)/shard_map/ppermute | solution.py:454
  36.2 0.7 collective-permute-start.4
  36.9 5.7 %stream_pass.3 = (f32[8,512,512]{2,1,0:T(8,128)}, bf16[4,512,512]{2,1,0:T(8,128)(2,1)}, bf16[4,512,512]{2,1,0:T(8,128)(2,1)}) custom-call(s32[8]{0:T(128)} %broadcast_xor_fusion.order_ref, bf16[256,512]{1,0:T(8,128)(2,1)} %near_ref.3, bf16[256,512]{1,0:T(8,128)(2,1)} %copy-done.3, f32[8,512,512]{2,1,0:T(8,128)} %bitcast.17, ...), custom_call_target="tpu_custom_call", output_to_operand_aliasing={{0}: (4, {})} | custom-call | flops 1073741824 | bytes 12582912 | tf_op jit(solution)/shard_map/stream_pass/pallas_call | solution.py:87
  42.6 2.3 %fusion.5 = (bf16[512,512]{1,0:T(8,128)(2,1)}, bf16[512,512]{1,0:T(8,128)(2,1)S(1)}) fusion(bf16[4,512,512]{2,1,0:T(8,128)(2,1)S(1)} %collective-permute-done.18, bf16[4,512,512]{2,1,0:T(8,128)(2,1)} %get-tuple-element.27), kind=kLoop, calls=%fused_computation.12 | loop fusion | flops 2097152 | bytes 3145728 | tf_op jit(solution)/shard_map/convert_element_type | solution.py:525
  44.8 1.3 %collective-permute-start.20 = (bf16[512,512]{1,0:T(8,128)(2,1)S(1)}, bf16[512,512]{1,0:T(8,128)(2,1)S(1)}, u32[]{:S(2)}, u32[]{:S(2)}) collective-permute-start(bf16[512,512]{1,0:T(8,128)(2,1)S(1)} %get-tuple-element.37), channel_id=1, source_target_pairs={{0,4},{1,5},{2,6},{3,7},{4,0},{5,1},{6,2},{7,3},{8,12},{9,13},{10,... | collective-permute-start | bytes 1572872 | tf_op jit(solution)/shard_map/ppermute | solution.py:454
  46.2 0.6 collective-permute-start.10
  46.8 0.7 collective-permute-start.6
  47.5 0.2 collective-permute-done.1.refs_8_.refs_0_
  47.7 1.4 %collective-permute-start.12 = (bf16[256,512]{1,0:T(8,128)(2,1)S(1)}, bf16[256,512]{1,0:T(8,128)(2,1)S(1)}, u32[]{:S(2)}, u32[]{:S(2)}) collective-permute-start(bf16[256,512]{1,0:T(8,128)(2,1)S(1)} %collective-permute-done.4.refs_2_), channel_id=1, source_target_pairs={{0,2},{1,3},{2,0},{3,1},{4,6},{5,7},{6,4},{7,5},{8,10},{9,11},{10,... | collective-permute-start | bytes 786440 | tf_op jit(solution)/shard_map/ppermute | solution.py:454
  49.1 6.4 %collective-permute-done.10.refs_5_ = bf16[256,512]{1,0:T(8,128)(2,1)S(1)} collective-permute-done((bf16[256,512]{1,0:T(8,128)(2,1)S(1)}, bf16[256,512]{1,0:T(8,128)(2,1)S(1)}, u32[]{:S(2)}, u32[]{:S(2)}) %collective-permute-start.10) | collective-permute-done | bytes 262176 | tf_op jit(solution)/shard_map/ppermute | solution.py:454
  55.5 8.4 %collective-permute-done.6.refs_3_ = bf16[256,512]{1,0:T(8,128)(2,1)} collective-permute-done((bf16[256,512]{1,0:T(8,128)(2,1)S(1)}, bf16[256,512]{1,0:T(8,128)(2,1)}, u32[]{:S(2)}, u32[]{:S(2)}) %collective-permute-start.6) | collective-permute-done | bytes 262176 | tf_op jit(solution)/shard_map/ppermute | solution.py:454
  63.9 0.6 collective-permute-start.11
  64.5 0.1 copy-done.10
  64.6 0.5 collective-permute-start.14
  65.1 2.0 %fusion = bf16[512,512]{1,0:T(8,128)(2,1)} fusion(bf16[512,512]{1,0:T(8,128)(2,1)S(1)} %collective-permute-done.20, bf16[4,512,512]{2,1,0:T(8,128)(2,1)S(1)} %collective-permute-done.18, bf16[4,512,512]{2,1,0:T(8,128)(2,1)} %get-tuple-element.27), kind=kLoop, calls=%fused_computation.2 | loop fusion | flops 1572864 | bytes 2097152 | tf_op jit(solution)/shard_map/convert_element_type | solution.py:525
  67.2 0.9 collective-permute-start.19
  68.0 1.5 %collective-permute-start.21 = (bf16[512,512]{1,0:T(8,128)(2,1)}, bf16[512,512]{1,0:T(8,128)(2,1)}, u32[]{:S(2)}, u32[]{:S(2)}) collective-permute-start(bf16[512,512]{1,0:T(8,128)(2,1)} %fusion), channel_id=1, source_target_pairs={{0,2},{1,3},{2,0},{3,1},{4,6},{5,7},{6,4},{7,5},{8,10},{9,11},{10,... | collective-permute-start | bytes 1572872 | tf_op jit(solution)/shard_map/ppermute | solution.py:454
  69.6 0.7 copy-done.11
  70.3 3.8 %collective-permute-done.14.refs_7_ = bf16[256,512]{1,0:T(8,128)(2,1)} collective-permute-done((bf16[256,512]{1,0:T(8,128)(2,1)}, bf16[256,512]{1,0:T(8,128)(2,1)}, u32[]{:S(2)}, u32[]{:S(2)}) %collective-permute-start.14) | collective-permute-done | bytes 262176 | tf_op jit(solution)/shard_map/ppermute | solution.py:454
  74.1 2.3 %turn_rows.1.refs_16_ = bf16[512,512]{1,0:T(8,128)(2,1)} custom-call(bf16[256,512]{1,0:T(8,128)(2,1)} %near_ref.3, bf16[256,512]{1,0:T(8,128)(2,1)} %copy-done.3, s32[1,512]{1,0:T(1,128)} %bitcast.21), custom_call_target="tpu_custom_call" | custom-call | flops 268435456 | bytes 1048576 | tf_op jit(solution)/shard_map/turn_rows/pallas_call | solution.py:147
  76.4 8.8 %update_tiles.1 = (f32[4096,512]{1,0:T(8,128)}, f32[24,128,128]{2,1,0:T(8,128)}, f32[24,128,128]{2,1,0:T(8,128)}, bf16[24,128,128]{2,1,0:T(8,128)(2,1)}) custom-call(s32[24]{0:T(128)} %get-tuple-element.42.refs_1_.owned, s32[24]{0:T(128)} %copy-done.17, s32[24]{0:T(128)} %fusion.10.refs_3_.piece, ...), custom_call_target="tpu_custom_call", output_to_operand_aliasing={{0}: (21, {})} | custom-call | flops 402653184 | bytes 10223616 | tf_op jit(solution)/shard_map/update_tiles/pallas_call | solution.py:272
  85.3 2.1 %collective-permute-start.24 = (bf16[24,128,128]{2,1,0:T(8,128)(2,1)}, bf16[24,128,128]{2,1,0:T(8,128)(2,1)}, u32[]{:S(2)}, u32[]{:S(2)}) collective-permute-start(bf16[24,128,128]{2,1,0:T(8,128)(2,1)} %get-tuple-element.31), channel_id=1, source_target_pairs={{0,16},{16,0},{1,17},{17,1},{2,18},{18,2},{3,19},{19,3},{4,20},{20... | collective-permute-start | bytes 2359304 | tf_op jit(solution)/shard_map/ppermute | solution.py:454
  87.4 1.6 %fusion.1 = f32[512,512]{1,0:T(8,128)S(1)} fusion(bf16[512,512]{1,0:T(8,128)(2,1)} %collective-permute-done.21, bf16[512,512]{1,0:T(8,128)(2,1)} %collective-permute-done.19, bf16[4,512,512]{2,1,0:T(8,128)(2,1)S(1)} %collective-permute-done.18, bf16[4,512,512]{2,1,0:T(8,128)(2,1)} %get-tuple-element.27), kind=kLoop, calls=%fused_computation.4 | loop fusion | flops 1835008 | bytes 3145728 | tf_op jit(solution)/shard_map/add | solution.py:526
  89.0 0.1 collective-permute-start.22
  89.1 10.6 %finish_state.2 = (f32[512,512]{1,0:T(8,128)}, f32[4096,512]{1,0:T(8,128)}) custom-call(s32[24]{0:T(128)} %get-tuple-element.42.refs_1_.owned, s32[24]{0:T(128)} %copy-done.17, bf16[256,512]{1,0:T(8,128)(2,1)} %copy-done.2, bf16[256,512]{1,0:T(8,128)(2,1)} %copy-done.6, bf16[256,512]{1,0:T(8,128)(2,1)} %copy-done.5, ...), custom_call_target="tpu_custom_call" | custom-call | flops 1073741824 | bytes 16777216 | tf_op jit(solution)/shard_map/finish_state/pallas_call | solution.py:440
  99.7 5.1 %turned_product.1 = (f32[256,512]{1,0:T(8,128)}, bf16[256,512]{1,0:T(8,128)(2,1)}) custom-call(bf16[256,512]{1,0:T(8,128)(2,1)} %copy-done.9, bf16[256,512]{1,0:T(8,128)(2,1)} %copy-done.10, bf16[256,512]{1,0:T(8,128)(2,1)} %copy-done.11, bf16[256,512]{1,0:T(8,128)(2,1)} %collective-permute-done.7.refs_11_.refs_3_, bf16[256,512]{1,0:T(8,128)(2,1)} %copy-done.12, ...), custom_call_target="tpu_custom_call" | custom-call | flops 1073741824 | bytes 4194304 | tf_op jit(solution)/shard_map/turned_product/pallas_call | solution.py:398
  104.9 2.0 %collective-permute-start.17 = (bf16[256,512]{1,0:T(8,128)(2,1)}, bf16[256,512]{1,0:T(8,128)(2,1)S(1)}, u32[]{:S(2)}, u32[]{:S(2)}) collective-permute-start(bf16[256,512]{1,0:T(8,128)(2,1)} %get-tuple-element.26), channel_id=1, source_target_pairs={{0,16},{16,0},{1,17},{17,1},{2,18},{18,2},{3,19},{19,3},{4,20},{20... | collective-permute-start | bytes 786440 | tf_op jit(solution)/shard_map/ppermute | solution.py:454
  106.9 4.7 %collective-permute-done.22 = bf16[256,512]{1,0:T(8,128)(2,1)S(1)} collective-permute-done((bf16[256,512]{1,0:T(8,128)(2,1)S(1)}, bf16[256,512]{1,0:T(8,128)(2,1)S(1)}, u32[]{:S(2)}, u32[]{:S(2)}) %collective-permute-start.22) | collective-permute-done | bytes 262176 | tf_op jit(solution)/shard_map/ppermute | solution.py:454
  111.6 4.6 %collective-permute-start.23 = (bf16[256,512]{1,0:T(8,128)(2,1)S(1)}, bf16[256,512]{1,0:T(8,128)(2,1)S(1)}, u32[]{:S(2)}, u32[]{:S(2)}) collective-permute-start(bf16[256,512]{1,0:T(8,128)(2,1)S(1)} %fusion.4), channel_id=1, source_target_pairs={{0,8},{1,9},{2,10},{3,11},{4,12},{5,13},{6,14},{7,15},{8,0},{9,1},... | collective-permute-start | bytes 786440 | tf_op jit(solution)/shard_map/ppermute | solution.py:454
  116.3 8.2 %finish_state.3 = f32[4096,512]{1,0:T(8,128)} custom-call(s32[24]{0:T(128)} %get-tuple-element.42.refs_1_.owned, s32[24]{0:T(128)} %copy-done.17, f32[4096,512]{1,0:T(8,128)} %a_ref.1, f32[24,128,128]{2,1,0:T(8,128)} %get-tuple-element.30.new_ref), custom_call_target="tpu_custom_call" | custom-call | bytes 16777216 | tf_op jit(solution)/shard_map/finish_state/pallas_call | solution.py:440
  124.5 0.8 add_convert_fusion.2
  125.3 2.3 %add.81 = bf16[24,128,128]{2,1,0:T(8,128)(2,1)} add(bf16[24,128,128]{2,1,0:T(8,128)(2,1)S(1)} %copy-done.14, bf16[24,128,128]{2,1,0:T(8,128)(2,1)} %collective-permute-done.24) | non-fusion elementwise | flops 393216 | bytes 2359296 | tf_op jit(solution)/shard_map/add | solution.py:538
  127.6 0.8 fusion.3
  (69 shorter events, 0.6 us)
Async XLA Ops:
  0.6 3.1 %copy-start = (s32[64,64]{1,0:T(8,128)S(1)}, s32[64,64]{1,0:T(8,128)}, u32[]{:S(2)}) copy-start(s32[64,64]{1,0:T(8,128)} %param.14) | copy-start | bytes 49156
  0.6 13.0 %collective-permute-start.16 = (bf16[256,512]{1,0:T(8,128)(2,1)}, bf16[256,512]{1,0:T(8,128)(2,1)S(1)}, u32[]{:S(2)}, u32[]{:S(2)}) collective-permute-start(bf16[256,512]{1,0:T(8,128)(2,1)} %near_ref.3), channel_id=1, source_target_pairs={{0,16},{16,0},{1,17},{17,1},{2,18},{18,2},{3,19},{19,3},{4,20},{20... | collective-permute-start | bytes 786440 | tf_op jit(solution)/shard_map/ppermute | solution.py:454
  7.2 1.9 %copy-start.17 = (s32[24]{0:T(128)}, s32[24]{0:T(128)S(1)}, u32[]{:S(2)}) copy-start(s32[24]{0:T(128)S(1)} %get-tuple-element.35.refs_2_.row) | copy-start | bytes 292
  13.7 0.7 copy-start.3
  14.4 4.9 %copy-start.16 = (bf16[256,512]{1,0:T(8,128)(2,1)S(1)}, bf16[256,512]{1,0:T(8,128)(2,1)}, u32[]{:S(2)}) copy-start(bf16[256,512]{1,0:T(8,128)(2,1)} %param.8) | copy-start | bytes 786436
  19.3 23.3 %collective-permute-start.18 = (bf16[4,512,512]{2,1,0:T(8,128)(2,1)}, bf16[4,512,512]{2,1,0:T(8,128)(2,1)S(1)}, u32[]{:S(2)}, u32[]{:S(2)}) collective-permute-start(bf16[4,512,512]{2,1,0:T(8,128)(2,1)} %back_product.1), channel_id=1, source_target_pairs={{0,1},{1,0},{2,3},{3,2},{4,5},{5,4},{6,7},{7,6},{8,9},{9,8},{10,11... | collective-permute-start | bytes 6291464 | tf_op jit(solution)/shard_map/ppermute | solution.py:454
  19.3 15.2 %collective-permute-start = (bf16[256,512]{1,0:T(8,128)(2,1)S(1)}, bf16[256,512]{1,0:T(8,128)(2,1)S(1)}, u32[]{:S(2)}, u32[]{:S(2)}) collective-permute-start(bf16[256,512]{1,0:T(8,128)(2,1)S(1)} %copy-done.16), channel_id=1, source_target_pairs={{0,8},{1,9},{2,10},{3,11},{4,12},{5,13},{6,14},{7,15},{8,0},{9,1},... | collective-permute-start | bytes 786440 | tf_op jit(solution)/shard_map/ppermute | solution.py:454
  34.6 11.6 %copy-start.2 = (bf16[256,512]{1,0:T(8,128)(2,1)}, bf16[256,512]{1,0:T(8,128)(2,1)S(1)}, u32[]{:S(2)}) copy-start(bf16[256,512]{1,0:T(8,128)(2,1)S(1)} %get-tuple-element.39.refs_0_) | copy-start | bytes 786436
  34.6 12.2 %collective-permute-start.8 = (bf16[256,512]{1,0:T(8,128)(2,1)S(1)}, bf16[256,512]{1,0:T(8,128)(2,1)S(1)}, u32[]{:S(2)}, u32[]{:S(2)}) collective-permute-start(bf16[256,512]{1,0:T(8,128)(2,1)S(1)} %get-tuple-element.39.refs_0_), channel_id=1, source_target_pairs={{0,2},{1,3},{2,0},{3,1},{4,6},{5,7},{6,4},{7,5},{8,10},{9,11},{10,... | collective-permute-start | bytes 786440 | tf_op jit(solution)/shard_map/ppermute | solution.py:454
  36.2 11.3 %collective-permute-start.4 = (bf16[256,512]{1,0:T(8,128)(2,1)S(1)}, bf16[256,512]{1,0:T(8,128)(2,1)S(1)}, u32[]{:S(2)}, u32[]{:S(2)}) collective-permute-start(bf16[256,512]{1,0:T(8,128)(2,1)S(1)} %get-tuple-element.39.refs_0_), channel_id=1, source_target_pairs={{0,4},{1,5},{2,6},{3,7},{4,0},{5,1},{6,2},{7,3},{8,12},{9,13},{10,... | collective-permute-start | bytes 786440 | tf_op jit(solution)/shard_map/ppermute | solution.py:454
  36.8 9.4 %collective-permute-start.2 = (bf16[256,512]{1,0:T(8,128)(2,1)S(1)}, bf16[256,512]{1,0:T(8,128)(2,1)S(1)}, u32[]{:S(2)}, u32[]{:S(2)}) collective-permute-start(bf16[256,512]{1,0:T(8,128)(2,1)S(1)} %get-tuple-element.38), channel_id=1, source_target_pairs={{0,16},{16,0},{1,17},{17,1},{2,18},{18,2},{3,19},{19,3},{4,20},{20... | collective-permute-start | bytes 786440 | tf_op jit(solution)/shard_map/ppermute | solution.py:454
  44.8 19.8 %collective-permute-start.20 = (bf16[512,512]{1,0:T(8,128)(2,1)S(1)}, bf16[512,512]{1,0:T(8,128)(2,1)S(1)}, u32[]{:S(2)}, u32[]{:S(2)}) collective-permute-start(bf16[512,512]{1,0:T(8,128)(2,1)S(1)} %get-tuple-element.37), channel_id=1, source_target_pairs={{0,4},{1,5},{2,6},{3,7},{4,0},{5,1},{6,2},{7,3},{8,12},{9,13},{10,... | collective-permute-start | bytes 1572872 | tf_op jit(solution)/shard_map/ppermute | solution.py:454
  46.2 1.5 %collective-permute-start.1 = (bf16[256,512]{1,0:T(8,128)(2,1)S(1)}, bf16[256,512]{1,0:T(8,128)(2,1)S(1)}, u32[]{:S(2)}, u32[]{:S(2)}) collective-permute-start(bf16[256,512]{1,0:T(8,128)(2,1)S(1)} %get-tuple-element.39.refs_0_), channel_id=1, source_target_pairs={{0,1},{1,0},{2,3},{3,2},{4,5},{5,4},{6,7},{7,6},{8,9},{9,8},{10,11... | collective-permute-start | bytes 786440 | tf_op jit(solution)/shard_map/ppermute | solution.py:454
  46.2 30.2 %copy-start.6 = (bf16[256,512]{1,0:T(8,128)(2,1)}, bf16[256,512]{1,0:T(8,128)(2,1)S(1)}, u32[]{:S(2)}) copy-start(bf16[256,512]{1,0:T(8,128)(2,1)S(1)} %collective-permute-done.2.refs_1_) | copy-start | bytes 786436
  46.2 9.2 %collective-permute-start.10 = (bf16[256,512]{1,0:T(8,128)(2,1)S(1)}, bf16[256,512]{1,0:T(8,128)(2,1)S(1)}, u32[]{:S(2)}, u32[]{:S(2)}) collective-permute-start(bf16[256,512]{1,0:T(8,128)(2,1)S(1)} %collective-permute-done.2.refs_1_), channel_id=1, source_target_pairs={{0,2},{1,3},{2,0},{3,1},{4,6},{5,7},{6,4},{7,5},{8,10},{9,11},{10,... | collective-permute-start | bytes 786440 | tf_op jit(solution)/shard_map/ppermute | solution.py:454
  46.8 29.6 %copy-start.4 = (bf16[256,512]{1,0:T(8,128)(2,1)}, bf16[256,512]{1,0:T(8,128)(2,1)S(1)}, u32[]{:S(2)}) copy-start(bf16[256,512]{1,0:T(8,128)(2,1)S(1)} %collective-permute-done.8.refs_4_) | copy-start | bytes 786436
  46.8 17.1 %collective-permute-start.6 = (bf16[256,512]{1,0:T(8,128)(2,1)S(1)}, bf16[256,512]{1,0:T(8,128)(2,1)}, u32[]{:S(2)}, u32[]{:S(2)}) collective-permute-start(bf16[256,512]{1,0:T(8,128)(2,1)S(1)} %collective-permute-done.2.refs_1_), channel_id=1, source_target_pairs={{0,4},{1,5},{2,6},{3,7},{4,0},{5,1},{6,2},{7,3},{8,12},{9,13},{10,... | collective-permute-start | bytes 786440 | tf_op jit(solution)/shard_map/ppermute | solution.py:454
  47.5 28.9 %copy-start.5 = (bf16[256,512]{1,0:T(8,128)(2,1)}, bf16[256,512]{1,0:T(8,128)(2,1)S(1)}, u32[]{:S(2)}) copy-start(bf16[256,512]{1,0:T(8,128)(2,1)S(1)} %collective-permute-done.4.refs_2_) | copy-start | bytes 786436
  47.5 16.4 %collective-permute-start.3 = (bf16[256,512]{1,0:T(8,128)(2,1)S(1)}, bf16[256,512]{1,0:T(8,128)(2,1)S(1)}, u32[]{:S(2)}, u32[]{:S(2)}) collective-permute-start(bf16[256,512]{1,0:T(8,128)(2,1)S(1)} %collective-permute-done.2.refs_1_), channel_id=1, source_target_pairs={{0,1},{1,0},{2,3},{3,2},{4,5},{5,4},{6,7},{7,6},{8,9},{9,8},{10,11... | collective-permute-start | bytes 786440 | tf_op jit(solution)/shard_map/ppermute | solution.py:454
  47.7 16.2 %copy-start.9 = (bf16[256,512]{1,0:T(8,128)(2,1)}, bf16[256,512]{1,0:T(8,128)(2,1)S(1)}, u32[]{:S(2)}) copy-start(bf16[256,512]{1,0:T(8,128)(2,1)S(1)} %collective-permute-done.1.refs_8_.refs_0_) | copy-start | bytes 786436
  47.7 20.3 %collective-permute-start.12 = (bf16[256,512]{1,0:T(8,128)(2,1)S(1)}, bf16[256,512]{1,0:T(8,128)(2,1)S(1)}, u32[]{:S(2)}, u32[]{:S(2)}) collective-permute-start(bf16[256,512]{1,0:T(8,128)(2,1)S(1)} %collective-permute-done.4.refs_2_), channel_id=1, source_target_pairs={{0,2},{1,3},{2,0},{3,1},{4,6},{5,7},{6,4},{7,5},{8,10},{9,11},{10,... | collective-permute-start | bytes 786440 | tf_op jit(solution)/shard_map/ppermute | solution.py:454
  55.5 21.0 %copy-start.7 = (bf16[256,512]{1,0:T(8,128)(2,1)}, bf16[256,512]{1,0:T(8,128)(2,1)S(1)}, u32[]{:S(2)}) copy-start(bf16[256,512]{1,0:T(8,128)(2,1)S(1)} %collective-permute-done.10.refs_5_) | copy-start | bytes 786436
  55.5 14.1 %collective-permute-start.5 = (bf16[256,512]{1,0:T(8,128)(2,1)S(1)}, bf16[256,512]{1,0:T(8,128)(2,1)S(1)}, u32[]{:S(2)}, u32[]{:S(2)}) collective-permute-start(bf16[256,512]{1,0:T(8,128)(2,1)S(1)} %collective-permute-done.4.refs_2_), channel_id=1, source_target_pairs={{0,1},{1,0},{2,3},{3,2},{4,5},{5,4},{6,7},{7,6},{8,9},{9,8},{10,11... | collective-permute-start | bytes 786440 | tf_op jit(solution)/shard_map/ppermute | solution.py:454
  63.9 3.3 %collective-permute-start.9 = (bf16[256,512]{1,0:T(8,128)(2,1)S(1)}, bf16[256,512]{1,0:T(8,128)(2,1)S(1)}, u32[]{:S(2)}, u32[]{:S(2)}) collective-permute-start(bf16[256,512]{1,0:T(8,128)(2,1)S(1)} %collective-permute-done.8.refs_4_), channel_id=1, source_target_pairs={{0,1},{1,0},{2,3},{3,2},{4,5},{5,4},{6,7},{7,6},{8,9},{9,8},{10,11... | collective-permute-start | bytes 786440 | tf_op jit(solution)/shard_map/ppermute | solution.py:454
  63.9 0.7 copy-start.10
  63.9 5.7 %collective-permute-start.11 = (bf16[256,512]{1,0:T(8,128)(2,1)S(1)}, bf16[256,512]{1,0:T(8,128)(2,1)S(1)}, u32[]{:S(2)}, u32[]{:S(2)}) collective-permute-start(bf16[256,512]{1,0:T(8,128)(2,1)S(1)} %collective-permute-done.10.refs_5_), channel_id=1, source_target_pairs={{0,1},{1,0},{2,3},{3,2},{4,5},{5,4},{6,7},{7,6},{8,9},{9,8},{10,11... | collective-permute-start | bytes 786440 | tf_op jit(solution)/shard_map/ppermute | solution.py:454
  64.6 9.5 %collective-permute-start.14 = (bf16[256,512]{1,0:T(8,128)(2,1)}, bf16[256,512]{1,0:T(8,128)(2,1)}, u32[]{:S(2)}, u32[]{:S(2)}) collective-permute-start(bf16[256,512]{1,0:T(8,128)(2,1)} %collective-permute-done.6.refs_3_), channel_id=1, source_target_pairs={{0,2},{1,3},{2,0},{3,1},{4,6},{5,7},{6,4},{7,5},{8,10},{9,11},{10,... | collective-permute-start | bytes 786440 | tf_op jit(solution)/shard_map/ppermute | solution.py:454
  67.2 3.1 %copy-start.12 = (bf16[256,512]{1,0:T(8,128)(2,1)}, bf16[256,512]{1,0:T(8,128)(2,1)S(1)}, u32[]{:S(2)}) copy-start(bf16[256,512]{1,0:T(8,128)(2,1)S(1)} %collective-permute-done.9.refs_12_.refs_4_) | copy-start | bytes 786436
  67.2 20.2 %collective-permute-start.19 = (bf16[512,512]{1,0:T(8,128)(2,1)}, bf16[512,512]{1,0:T(8,128)(2,1)}, u32[]{:S(2)}, u32[]{:S(2)}) collective-permute-start(bf16[512,512]{1,0:T(8,128)(2,1)} %get-tuple-element.36), channel_id=1, source_target_pairs={{0,4},{1,5},{2,6},{3,7},{4,0},{5,1},{6,2},{7,3},{8,12},{9,13},{10,... | collective-permute-start | bytes 1572872 | tf_op jit(solution)/shard_map/ppermute | solution.py:454
  68.0 8.4 %copy-start.8 = (bf16[256,512]{1,0:T(8,128)(2,1)}, bf16[256,512]{1,0:T(8,128)(2,1)S(1)}, u32[]{:S(2)}) copy-start(bf16[256,512]{1,0:T(8,128)(2,1)S(1)} %collective-permute-done.12.refs_6_) | copy-start | bytes 786436
  68.0 19.3 %collective-permute-start.21 = (bf16[512,512]{1,0:T(8,128)(2,1)}, bf16[512,512]{1,0:T(8,128)(2,1)}, u32[]{:S(2)}, u32[]{:S(2)}) collective-permute-start(bf16[512,512]{1,0:T(8,128)(2,1)} %fusion), channel_id=1, source_target_pairs={{0,2},{1,3},{2,0},{3,1},{4,6},{5,7},{6,4},{7,5},{8,10},{9,11},{10,... | collective-permute-start | bytes 1572872 | tf_op jit(solution)/shard_map/ppermute | solution.py:454
  69.6 0.7 copy-start.11
  69.6 6.8 %collective-permute-start.7 = (bf16[256,512]{1,0:T(8,128)(2,1)}, bf16[256,512]{1,0:T(8,128)(2,1)}, u32[]{:S(2)}, u32[]{:S(2)}) collective-permute-start(bf16[256,512]{1,0:T(8,128)(2,1)} %collective-permute-done.6.refs_3_), channel_id=1, source_target_pairs={{0,1},{1,0},{2,3},{3,2},{4,5},{5,4},{6,7},{7,6},{8,9},{9,8},{10,11... | collective-permute-start | bytes 786440 | tf_op jit(solution)/shard_map/ppermute | solution.py:454
  70.3 3.8 %copy-start.13 = (bf16[256,512]{1,0:T(8,128)(2,1)}, bf16[256,512]{1,0:T(8,128)(2,1)S(1)}, u32[]{:S(2)}) copy-start(bf16[256,512]{1,0:T(8,128)(2,1)S(1)} %collective-permute-done.11.refs_13_.refs_5_) | copy-start | bytes 786436
  70.3 6.1 %collective-permute-start.13 = (bf16[256,512]{1,0:T(8,128)(2,1)S(1)}, bf16[256,512]{1,0:T(8,128)(2,1)}, u32[]{:S(2)}, u32[]{:S(2)}) collective-permute-start(bf16[256,512]{1,0:T(8,128)(2,1)S(1)} %collective-permute-done.12.refs_6_), channel_id=1, source_target_pairs={{0,1},{1,0},{2,3},{3,2},{4,5},{5,4},{6,7},{7,6},{8,9},{9,8},{10,11... | collective-permute-start | bytes 786440 | tf_op jit(solution)/shard_map/ppermute | solution.py:454
  74.1 2.3 %collective-permute-start.15 = (bf16[256,512]{1,0:T(8,128)(2,1)}, bf16[256,512]{1,0:T(8,128)(2,1)}, u32[]{:S(2)}, u32[]{:S(2)}) collective-permute-start(bf16[256,512]{1,0:T(8,128)(2,1)} %collective-permute-done.14.refs_7_), channel_id=1, source_target_pairs={{0,1},{1,0},{2,3},{3,2},{4,5},{5,4},{6,7},{7,6},{8,9},{9,8},{10,11... | collective-permute-start | bytes 786440 | tf_op jit(solution)/shard_map/ppermute | solution.py:454
  85.3 40.0 %collective-permute-start.24 = (bf16[24,128,128]{2,1,0:T(8,128)(2,1)}, bf16[24,128,128]{2,1,0:T(8,128)(2,1)}, u32[]{:S(2)}, u32[]{:S(2)}) collective-permute-start(bf16[24,128,128]{2,1,0:T(8,128)(2,1)} %get-tuple-element.31), channel_id=1, source_target_pairs={{0,16},{16,0},{1,17},{17,1},{2,18},{18,2},{3,19},{19,3},{4,20},{20... | collective-permute-start | bytes 2359304 | tf_op jit(solution)/shard_map/ppermute | solution.py:454
  89.0 22.6 %collective-permute-start.22 = (bf16[256,512]{1,0:T(8,128)(2,1)S(1)}, bf16[256,512]{1,0:T(8,128)(2,1)S(1)}, u32[]{:S(2)}, u32[]{:S(2)}) collective-permute-start(bf16[256,512]{1,0:T(8,128)(2,1)S(1)} %slice.69), channel_id=1, source_target_pairs={{0,16},{16,0},{1,17},{17,1},{2,18},{18,2},{3,19},{19,3},{4,20},{20... | collective-permute-start | bytes 786440 | tf_op jit(solution)/shard_map/ppermute | solution.py:454
  104.9 19.6 %collective-permute-start.17 = (bf16[256,512]{1,0:T(8,128)(2,1)}, bf16[256,512]{1,0:T(8,128)(2,1)S(1)}, u32[]{:S(2)}, u32[]{:S(2)}) collective-permute-start(bf16[256,512]{1,0:T(8,128)(2,1)} %get-tuple-element.26), channel_id=1, source_target_pairs={{0,16},{16,0},{1,17},{17,1},{2,18},{18,2},{3,19},{19,3},{4,20},{20... | collective-permute-start | bytes 786440 | tf_op jit(solution)/shard_map/ppermute | solution.py:454
  111.6 15.9 %collective-permute-start.23 = (bf16[256,512]{1,0:T(8,128)(2,1)S(1)}, bf16[256,512]{1,0:T(8,128)(2,1)S(1)}, u32[]{:S(2)}, u32[]{:S(2)}) collective-permute-start(bf16[256,512]{1,0:T(8,128)(2,1)S(1)} %fusion.4), channel_id=1, source_target_pairs={{0,8},{1,9},{2,10},{3,11},{4,12},{5,13},{6,14},{7,15},{8,0},{9,1},... | collective-permute-start | bytes 786440 | tf_op jit(solution)/shard_map/ppermute | solution.py:454
  116.3 8.2 %copy-start.15 = (f32[256,512]{1,0:T(8,128)S(1)}, f32[256,512]{1,0:T(8,128)}, u32[]{:S(2)}) copy-start(f32[256,512]{1,0:T(8,128)} %get-tuple-element.25) | copy-start | bytes 1572868
  116.3 9.0 %copy-start.14 = (bf16[24,128,128]{2,1,0:T(8,128)(2,1)S(1)}, bf16[24,128,128]{2,1,0:T(8,128)(2,1)}, u32[]{:S(2)}) copy-start(bf16[24,128,128]{2,1,0:T(8,128)(2,1)} %get-tuple-element.31) | copy-start | bytes 2359300
  124.5 3.9 %copy-start.1 = (s32[64,64]{1,0:T(8,128)S(1)}, s32[64,64]{1,0:T(8,128)}, u32[]{:S(2)}) copy-start(s32[64,64]{1,0:T(8,128)} %param.14) | copy-start | bytes 49156
